TPU v7x, 256 devices: a whole 4x4x8 slice. The times are simulated.
256 devices in a mesh: dp: 16 (over z_hi, x, core), row: 4 (over y), col: 4 (over z_lo).
Axes of the slice: x: 4, y: 4, z: 8 (z_hi: 2, z_lo: 4; z = z_hi * 4 + z_lo), core: 2. Of those that a mesh axis runs over, the one named last changes fastest.
Arguments:
- grad_parts: float32 [16, 2, 4096, 5120], P('dp', None, 'row', 'col'), may hold values from -5 to 5
- weight: float32 [2, 4096, 5120], P(None, ('row', 'dp'), 'col'), may hold values from -6 to 6
- row_state: float32 [2, 4096], P(None, ('row', 'dp')), may hold values from 0.3 to 8, as said below
- col_state: float32 [2, 5120], P(None, 'col'), may hold values from 0.05 to 0.5
Outputs:
- new_weight: float32 [2, 4096, 5120], P(None, 'row', 'col')
- new_row_state: float32 [2, 4096], P(None, ('row', 'dp'))
- new_col_state: float32 [2, 5120], P(None, 'col')
Inputs may be any that keep to these rules, and one draw needn't show every extreme that they name: `row_state`: positive row moments.
All inputs are finite; a program needn't handle non-finite values.
Results may differ from a plain program's by a relative error of at most 0.00002.
Values sent between devices are 32-bit elements; how exact they have to be, the bound alone decides.
No kernel may reach another device: no remote copies, remote signals or barrier semaphores. Data moves between devices by JAX's collectives and lax.ppermute only.
A program may use at most 128 MiB of HBM per device.

v0:
```python
import functools

import jax
import jax.numpy as jnp
from jax import lax
from jax.experimental import pallas as pl
from jax.experimental.pallas import tpu as pltpu
from jax.sharding import PartitionSpec as P

D = 4096
FF = 5120
E = 2
ROWS = 64
COLS = 1280
DECAY = 1.0 - 2.0 ** (-0.8)

DP = [(zh, x, c) for zh in range(2) for x in range(4) for c in range(2)]


def at(zh, x, c):
    return (zh % 2) * 8 + (x % 4) * 2 + c % 2


def dp_perm(dz, dx, dc):
    return [(at(zh, x, c), at(zh + dz, x + dx, c + dc)) for zh, x, c in DP]


CORE = dp_perm(0, 0, 1)
PLUS = dp_perm(0, 1, 0)
MINUS = dp_perm(0, -1, 0)
ZHALF = dp_perm(1, 0, 0)
FAR = dp_perm(0, 2, 0)


def send(value, perm):
    return lax.ppermute(value, "dp", perm)


def sum4(value, axis, perms):
    second, third, fourth = (lax.ppermute(value, axis, perm) for perm in perms)
    return (value + third) + (second + fourth)


RING4 = [[(i, (i + k) % 4) for i in range(4)] for k in (1, 2, 3)]
X4 = [dp_perm(0, k, 0) for k in (1, 2, 3)]


def place():
    dp = lax.axis_index("dp")
    return dp // 8, dp // 2 % 4, dp % 2


def after(values, *earlier):
    return lax.optimization_barrier((values, earlier))[0]


def cut(parts, start, size):
    return lax.dynamic_slice(parts, (*start, 0, 0), (*size, ROWS, COLS))


def scatter(parts):
    zh, x, c = place()
    high, low = x // 2, x % 2

    def swap(start, size, *earlier):
        core = after(1 - c, *earlier) if earlier else 1 - c
        return send(cut(parts, (*start, core), (*size, 1)), CORE)

    def block(theirs, expert, half, dx):
        to = (x + dx) % 4
        mine = cut(parts, (expert, half, to // 2, to % 2, c), (1,) * 5)
        return mine.reshape(ROWS, COLS) + theirs.reshape(ROWS, COLS)

    def block_pair(theirs, half, dxs):
        return [block(theirs[e], e, half, dxs[e]) for e in range(E)]

    def sides(swap, half, swapped):
        pick = lambda e, dx: lax.dynamic_index_in_dim(swap[e, 0], (x + dx) % 4 // 2, 0)
        order = (1, 0) if swapped else (0, 1)
        return [block(pick(e, dx), e, half, dx) for e, dx in zip(order, (1, 3))]

    def pair_send(pair):
        return [send(pair[0], PLUS), send(pair[1], MINUS)]

    def finish(far, side_swap, own_swap, half):
        near_rows = sides(side_swap, half, True)
        next_rows = sides(side_swap, half, False)
        rows = after(
            [jnp.concatenate([n, m + f]) for n, m, f in zip(near_rows, next_rows, far)]
        )
        got = pair_send(rows)
        own = block_pair(own_swap, half, (0, 0))
        total = [own[e] + got[1 - e][:ROWS] + got[e][ROWS:] for e in range(E)]
        return rows, after(jnp.stack(total))

    far_a = swap((0, 1 - zh, 1 - high, low), (E, 1, 1, 1))
    far_rows = after(block_pair(far_a, 1 - zh, (2, 2)))
    far = pair_send(far_rows)
    side_a = swap((0, 1 - zh, 0, 1 - low), (E, 1, 2, 1), far_rows)
    own_a = swap((0, 1 - zh, high, low), (E, 1, 1, 1), far_rows)
    rows, away = finish(far, side_a, own_a, 1 - zh)

    def both_experts(dx):
        to = (x + dx) % 4
        start = (0, zh, to // 2, to % 2)
        theirs = swap(start, (E, 1, 1, 1), rows)
        mine = cut(parts, (*start, c), (E, 1, 1, 1, 1))
        return (mine + theirs).reshape(E, ROWS, COLS)

    *terms, own = after([both_experts(dx) for dx in (1, 3, 2, 0)], rows)
    *terms, away = lax.optimization_barrier((*terms, away))
    other = send(away, ZHALF)
    got = [send(term, perm) for term, perm in zip(terms, (PLUS, MINUS, FAR))]
    return own + got[0] + got[1] + got[2] + other


def statistics(grad, weight, row_state, col_state):
    sq = grad * grad + 1e-30
    row_total = sum4(jnp.sum(sq, axis=2), "col", RING4)
    row = DECAY * row_state + (1.0 - DECAY) * row_total / FF
    sums = jnp.concatenate(
        [
            jnp.sum(sq, axis=1),
            jnp.sum(grad * grad / row[:, :, None], axis=1),
            jnp.sum(weight * weight, axis=1),
            jnp.broadcast_to(jnp.sum(row, axis=1)[:, None], (E, COLS)),
        ]
    )
    sums = sum4(sums, "dp", X4)
    sums = sum4(sums, "row", RING4)
    for perm in (CORE, ZHALF):
        sums = sums + send(sums, perm)
    squares, scaled, weights, rows = (sums[E * i : E * i + E] for i in range(4))
    col = DECAY * col_state + (1.0 - DECAY) * squares / D
    row_mean = rows[:, 0] / D
    scalars = jnp.stack([jnp.sum(scaled / col, axis=1), jnp.sum(weights, axis=1)])
    scalars = sum4(scalars, "col", RING4)
    clip = jnp.maximum(1.0, jnp.sqrt(scalars[0] * row_mean / (D * FF)))
    step = 0.3 * jnp.maximum(0.001, jnp.sqrt(scalars[1] / (D * FF)))
    return row, col, row_mean, step / clip


def place_kernel(slabs, where, *refs):
    *arrays, out, held, loaded, stored = refs
    copies = []
    at_row = 0
    for i, (array, start, size) in enumerate(slabs):
        stage = held.at[pl.ds(at_row, size)]
        at_row += size
        target = out.at[pl.ds(pl.multiple_of(where[i], 32), size)]
        copies.append(
            (
                pltpu.make_async_copy(arrays[array].at[pl.ds(start, size)], stage, loaded.at[i]),
                pltpu.make_async_copy(stage, target, stored.at[i]),
            )
        )
    for load, _ in copies:
        load.start()
    for load, store in copies:
        load.wait()
        store.start()
    for _, store in copies:
        store.wait()


def put(out, arrays, slabs, rows):
    any_space = pl.BlockSpec(memory_space=pl.ANY)
    operands = [jnp.stack(rows).astype(jnp.int32)]
    operands += [array.reshape(-1, COLS) for array in arrays]
    aliases = {}
    if out is not None:
        aliases = {len(operands): 0}
        operands.append(out)
    specs = [pl.BlockSpec(memory_space=pltpu.SMEM)] + [any_space] * (len(operands) - 1)
    return pl.pallas_call(
        functools.partial(place_kernel, slabs),
        out_shape=jax.ShapeDtypeStruct((E * 1024, COLS), jnp.float32),
        in_specs=specs,
        out_specs=any_space,
        scratch_shapes=[
            pltpu.VMEM((sum(size for _, _, size in slabs), COLS), jnp.float32),
            pltpu.SemaphoreType.DMA((len(slabs),)),
            pltpu.SemaphoreType.DMA((len(slabs),)),
        ],
        input_output_aliases=aliases,
    )(*operands)


def gather_rows(shard):
    zh, x, c = place()
    half = ROWS // 2

    def row(dc, expert, dz, dx, first=0):
        at_c = (zh + dz) % 2 * 8 + (x + dx) % 4 * 2 + (c + dc) % 2
        return expert * 1024 + ROWS * at_c + first

    def write(out, pieces):
        arrays, slabs, rows = [], [], []
        for mine, theirs, parts in pieces:
            for dc, array in enumerate((mine, theirs)):
                start = 0
                for size, *to in parts:
                    slabs.append((len(arrays), start, size))
                    rows.append(row(dc, *to))
                    start += size
                arrays.append(array)
        return put(out, arrays, slabs, rows)

    other = [send(shard[e], ZHALF) for e in range(E)]
    left, right = send(shard, PLUS), send(shard, MINUS)
    shard_c = send(shard, CORE)

    left, right, other_0, shard_c = lax.optimization_barrier((left, right, other[0], shard_c))
    plus = jnp.concatenate([left[0], other_0])
    minus = jnp.concatenate([right[1], other_0])
    plus, minus = lax.optimization_barrier((plus, minus))
    from_left, from_right = send(plus, PLUS), send(minus, MINUS)
    left_c, right_c = send(left, CORE), send(right, CORE)

    from_left, from_right, other_1, left_c, right_c = lax.optimization_barrier(
        (from_left, from_right, other[1], left_c, right_c)
    )
    plus = jnp.concatenate([other_1, from_left[ROWS : ROWS + half]])
    minus = jnp.concatenate([other_1, from_right[ROWS + half :]])
    plus, minus = lax.optimization_barrier((plus, minus))
    last_left, last_right = send(plus, PLUS), send(minus, MINUS)
    far_1 = send(other_1, FAR)
    from_left_c, from_right_c = send(from_left, CORE), send(from_right, CORE)
    others = jnp.concatenate([other_0, other_1])
    both = lambda dz, dx: [(ROWS, e, dz, dx) for e in range(E)]
    out = write(
        None,
        [
            (shard, shard_c, both(0, 0)),
            (left, left_c, both(0, 3)),
            (right, right_c, both(0, 1)),
            (from_left, from_left_c, [(ROWS, 0, 0, 2), (ROWS, 0, 1, 3)]),
            (from_right, from_right_c, [(ROWS, 1, 0, 2), (ROWS, 0, 1, 1)]),
        ],
    )

    out, last_left, last_right, far_1, others = lax.optimization_barrier(
        (out, last_left, last_right, far_1, others)
    )
    return write(
        out,
        [
            (others, send(others, CORE), both(1, 0)),
            (last_left, send(last_left, CORE), [(ROWS, 1, 1, 3), (half, 0, 1, 2, 0)]),
            (last_right, send(last_right, CORE), [(ROWS, 1, 1, 1), (half, 0, 1, 2, half)]),
            (far_1, send(far_1, CORE), [(ROWS, 1, 1, 2)]),
        ],
    )


def body(grad_parts, weight, row_state, col_state):
    grad = scatter(grad_parts.reshape(E, 2, 2, 2, 2, ROWS, COLS))
    row, col, row_mean, scale = statistics(grad, weight, row_state, col_state)
    vhat = row[:, :, None] * col[:, None, :] / row_mean[:, None, None]
    new = weight - scale[:, None, None] * (grad / jnp.sqrt(vhat))
    return gather_rows(new).reshape(E, 1024, COLS), row, col


def solution(mesh):
    placed = (
        P("dp", None, "row", "col"),
        P(None, ("row", "dp"), "col"),
        P(None, ("row", "dp")),
        P(None, "col"),
    )
    return jax.shard_map(
        body,
        mesh=mesh,
        in_specs=placed,
        out_specs=(P(None, "row", "col"), P(None, ("row", "dp")), P(None, "col")),
        check_vma=False,
    )
```

profile of v0, /device:TPU:1, one launch (start us, length us, event | category | flops | bytes accessed | tf_op | source)
XLA Modules:
  0.0 206.1 jit_solution(11358334297652912351)
XLA Ops:
  1.9 3.3 %collective-permute-start = (f32[2,1,1,1,1,64,1280]{6,5,4,3,2,1,0:T(8,128)S(1)}, f32[2,1,1,1,1,64,1280]{6,5,4,3,2,1,0:T(8,128)S(1)}, u32[]{:S(2)}, u32[]{:S(2)}) collective-permute-start(f32[2,1,1,1,1,64,1280]{6,5,4,3,2,1,0:T(8,128)S(1)} %constant_dynamic-slice_fusion.3), channel_id=1, source_target_pairs={{0,16},{16,0},{32,48},{48,32},{64,80},{80,64},{96,112},{112,96},{1... | collective-permute-start | bytes 1966088 | tf_op jit(solution)/shard_map/ppermute | solution.py:36
  10.0 2.7 %collective-permute-start.3 = (f32[64,1280]{1,0:T(8,128)S(1)}, f32[64,1280]{1,0:T(8,128)S(1)}, u32[]{:S(2)}, u32[]{:S(2)}) collective-permute-start(f32[64,1280]{1,0:T(8,128)S(1)} %get-tuple-element.36), channel_id=1, source_target_pairs={{0,96},{16,112},{32,0},{48,16},{64,32},{80,48},{96,64},{112,80},{1... | collective-permute-start | bytes 983048 | tf_op jit(solution)/shard_map/ppermute | solution.py:36
  13.9 6.3 %collective-permute-done.2 = f32[64,1280]{1,0:T(8,128)S(1)} collective-permute-done((f32[64,1280]{1,0:T(8,128)S(1)}, f32[64,1280]{1,0:T(8,128)S(1)}, u32[]{:S(2)}, u32[]{:S(2)}) %collective-permute-start.2) | collective-permute-done | bytes 327712 | tf_op jit(solution)/shard_map/ppermute | solution.py:36
  23.9 2.8 %collective-permute-start.9 = (f32[128,1280]{1,0:T(8,128)S(1)}, f32[128,1280]{1,0:T(8,128)S(1)}, u32[]{:S(2)}, u32[]{:S(2)}) collective-permute-start(f32[128,1280]{1,0:T(8,128)S(1)} %get-tuple-element.39), channel_id=1, source_target_pairs={{0,96},{16,112},{32,0},{48,16},{64,32},{80,48},{96,64},{112,80},{1... | collective-permute-start | bytes 1966088 | tf_op jit(solution)/shard_map/ppermute | solution.py:36
  30.0 11.3 %collective-permute-done.10 = f32[128,1280]{1,0:T(8,128)S(1)} collective-permute-done((f32[128,1280]{1,0:T(8,128)S(1)}, f32[128,1280]{1,0:T(8,128)S(1)}, u32[]{:S(2)}, u32[]{:S(2)}) %collective-permute-start.10) | collective-permute-done | bytes 655392 | tf_op jit(solution)/shard_map/ppermute | solution.py:36
  48.5 5.2 %collective-permute-start.14 = (f32[2,64,1280]{2,1,0:T(8,128)S(1)}, f32[2,64,1280]{2,1,0:T(8,128)S(1)}, u32[]{:S(2)}, u32[]{:S(2)}) collective-permute-start(f32[2,64,1280]{2,1,0:T(8,128)S(1)} %pad_maximum_fusion.4), channel_id=1, source_target_pairs={{0,128},{16,144},{32,160},{48,176},{64,192},{80,208},{96,224},{112... | collective-permute-start | bytes 1966088 | tf_op jit(solution)/shard_map/ppermute | solution.py:36
  53.7 10.0 %collective-permute-done.11 = f32[2,64,1280]{2,1,0:T(8,128)S(1)} collective-permute-done((f32[2,64,1280]{2,1,0:T(8,128)S(1)}, f32[2,64,1280]{2,1,0:T(8,128)S(1)}, u32[]{:S(2)}, u32[]{:S(2)}) %collective-permute-start.11) | collective-permute-done | bytes 655392 | tf_op jit(solution)/shard_map/ppermute | solution.py:36
  63.7 12.7 %collective-permute-done.13 = f32[2,64,1280]{2,1,0:T(8,128)S(1)} collective-permute-done((f32[2,64,1280]{2,1,0:T(8,128)S(1)}, f32[2,64,1280]{2,1,0:T(8,128)S(1)}, u32[]{:S(2)}, u32[]{:S(2)}) %collective-permute-start.13) | collective-permute-done | bytes 655392 | tf_op jit(solution)/shard_map/ppermute | solution.py:36
  76.7 2.8 %collective-permute-start.17 = (f32[2,64]{1,0:T(2,128)S(1)}, f32[2,64]{1,0:T(2,128)S(1)}, u32[]{:S(2)}, u32[]{:S(2)}) collective-permute-start(f32[2,64]{1,0:T(2,128)S(1)} %get-tuple-element.74), channel_id=1, source_target_pairs={{0,3},{1,0},{2,1},{3,2},{4,7},{5,4},{6,5},{7,6},{8,11},{9,8},{10,9... | collective-permute-start | bytes 1544 | tf_op jit(solution)/shard_map/ppermute | solution.py:40
  79.5 2.8 %collective-permute-start.16 = (f32[2,64]{1,0:T(2,128)S(1)}, f32[2,64]{1,0:T(2,128)S(1)}, u32[]{:S(2)}, u32[]{:S(2)}) collective-permute-start(f32[2,64]{1,0:T(2,128)S(1)} %get-tuple-element.74), channel_id=1, source_target_pairs={{0,1},{1,2},{2,3},{3,0},{4,5},{5,6},{6,7},{7,4},{8,9},{9,10},{10,1... | collective-permute-start | bytes 1544 | tf_op jit(solution)/shard_map/ppermute | solution.py:40
  82.3 3.3 %collective-permute-start.15 = (f32[2,64]{1,0:T(2,128)S(1)}, f32[2,64]{1,0:T(2,128)S(1)}, u32[]{:S(2)}, u32[]{:S(2)}) collective-permute-start(f32[2,64]{1,0:T(2,128)S(1)} %get-tuple-element.74), channel_id=1, source_target_pairs={{0,2},{1,3},{2,0},{3,1},{4,6},{5,7},{6,4},{7,5},{8,10},{9,11},{10,... | collective-permute-start | bytes 1544 | tf_op jit(solution)/shard_map/ppermute | solution.py:40
  94.1 2.9 %collective-permute-start.23 = (f32[8,1280]{1,0:T(8,128)S(1)}, f32[8,1280]{1,0:T(8,128)S(1)}, u32[]{:S(2)}, u32[]{:S(2)}) collective-permute-start(f32[8,1280]{1,0:T(8,128)S(1)} %add_add_fusion.2), channel_id=1, source_target_pairs={{0,12},{4,0},{8,4},{12,8},{1,13},{5,1},{9,5},{13,9},{2,14},{6,2},{... | collective-permute-start | bytes 122888 | tf_op jit(solution)/shard_map/ppermute | solution.py:40
  98.7 2.9 %collective-permute-done.22 = f32[8,1280]{1,0:T(8,128)S(1)} collective-permute-done((f32[8,1280]{1,0:T(8,128)S(1)}, f32[8,1280]{1,0:T(8,128)S(1)}, u32[]{:S(2)}, u32[]{:S(2)}) %collective-permute-start.22) | collective-permute-done | bytes 40992 | tf_op jit(solution)/shard_map/ppermute | solution.py:40
  101.6 6.3 %collective-permute-start.24 = (f32[8,1280]{1,0:T(8,128)S(1)}, f32[8,1280]{1,0:T(8,128)S(1)}, u32[]{:S(2)}, u32[]{:S(2)}) collective-permute-start(f32[8,1280]{1,0:T(8,128)S(1)} %add_add_fusion.1), channel_id=1, source_target_pairs={{0,16},{16,0},{32,48},{48,32},{64,80},{80,64},{96,112},{112,96},{1... | collective-permute-start | bytes 122888 | tf_op jit(solution)/shard_map/ppermute | solution.py:36
  108.7 5.6 %collective-permute-start.25 = (f32[8,1280]{1,0:T(8,128)S(1)}, f32[8,1280]{1,0:T(8,128)S(1)}, u32[]{:S(2)}, u32[]{:S(2)}) collective-permute-start(f32[8,1280]{1,0:T(8,128)S(1)} %add.813), channel_id=1, source_target_pairs={{0,128},{16,144},{32,160},{48,176},{64,192},{80,208},{96,224},{112... | collective-permute-start | bytes 122888 | tf_op jit(solution)/shard_map/ppermute | solution.py:36
  123.0 3.2 %collective-permute-start.32 = (f32[2,64,1280]{2,1,0:T(8,128)S(1)}, f32[2,64,1280]{2,1,0:T(8,128)S(1)}, u32[]{:S(2)}, u32[]{:S(2)}) collective-permute-start(f32[2,64,1280]{2,1,0:T(8,128)S(1)} %multiply_subtract_fusion), channel_id=1, source_target_pairs={{0,16},{16,0},{32,48},{48,32},{64,80},{80,64},{96,112},{112,96},{1... | collective-permute-start | bytes 1966088 | tf_op jit(solution)/shard_map/ppermute | solution.py:36
  127.8 6.2 %collective-permute-start.31 = (f32[64,1280]{1,0:T(8,128)S(1)}, f32[64,1280]{1,0:T(8,128)S(1)}, u32[]{:S(2)}, u32[]{:S(2)}) collective-permute-start(f32[64,1280]{1,0:T(8,128)S(1)} %get-tuple-element.95), channel_id=1, source_target_pairs={{0,128},{16,144},{32,160},{48,176},{64,192},{80,208},{96,224},{112... | collective-permute-start | bytes 983048 | tf_op jit(solution)/shard_map/ppermute | solution.py:36
  133.9 12.5 %collective-permute-done.31 = f32[64,1280]{1,0:T(8,128)S(1)} collective-permute-done((f32[64,1280]{1,0:T(8,128)S(1)}, f32[64,1280]{1,0:T(8,128)S(1)}, u32[]{:S(2)}, u32[]{:S(2)}) %collective-permute-start.31) | collective-permute-done | bytes 327712 | tf_op jit(solution)/shard_map/ppermute | solution.py:36
  152.3 5.3 %collective-permute-start.35 = (f32[64,1280]{1,0:T(8,128)S(1)}, f32[64,1280]{1,0:T(8,128)S(1)}, u32[]{:S(2)}, u32[]{:S(2)}) collective-permute-start(f32[64,1280]{1,0:T(8,128)S(1)} %get-tuple-element.94), channel_id=1, source_target_pairs={{0,128},{16,144},{32,160},{48,176},{64,192},{80,208},{96,224},{112... | collective-permute-start | bytes 983048 | tf_op jit(solution)/shard_map/ppermute | solution.py:36
  157.6 9.3 %collective-permute-done.35 = f32[64,1280]{1,0:T(8,128)S(1)} collective-permute-done((f32[64,1280]{1,0:T(8,128)S(1)}, f32[64,1280]{1,0:T(8,128)S(1)}, u32[]{:S(2)}, u32[]{:S(2)}) %collective-permute-start.35) | collective-permute-done | bytes 327712 | tf_op jit(solution)/shard_map/ppermute | solution.py:36
  168.1 3.6 %collective-permute-start.38 = (f32[128,1280]{1,0:T(8,128)}, f32[128,1280]{1,0:T(8,128)}, u32[]{:S(2)}, u32[]{:S(2)}) collective-permute-start(f32[128,1280]{1,0:T(8,128)} %collective-permute-done.33.refs_6_), channel_id=1, source_target_pairs={{0,16},{16,0},{32,48},{48,32},{64,80},{80,64},{96,112},{112,96},{1... | collective-permute-start | bytes 1966088 | tf_op jit(solution)/shard_map/ppermute | solution.py:36
  177.2 6.3 %shard_map.67.refs_8_ = f32[2048,1280]{1,0:T(8,128)} custom-call(s32[20]{0:T(128)} %stack.161.where, f32[128,1280]{1,0:T(8,128)} %bitcast.122, f32[128,1280]{1,0:T(8,128)} %bitcast.125, f32[128,1280]{1,0:T(8,128)} %bitcast.124, f32[128,1280]{1,0:T(8,128)} %bitcast.126, f32[128,1280]{1,0:T(8,128)} %bitcast.123, f32[128,1280]{1,0:T(8,128)} %bitcast.62.refs_5_, ...), custom_call_target="tpu_custom_call" | custom-call | tf_op jit(solution)/shard_map/pallas_call | solution.py:175
  183.5 10.0 %collective-permute-done.42.refs_6_ = f32[64,1280]{1,0:T(8,128)} collective-permute-done((f32[64,1280]{1,0:T(8,128)S(1)}, f32[64,1280]{1,0:T(8,128)}, u32[]{:S(2)}, u32[]{:S(2)}) %collective-permute-start.42) | collective-permute-done | bytes 327712 | tf_op jit(solution)/shard_map/ppermute | solution.py:36
  201.7 4.2 %shard_map.68 = f32[2048,1280]{1,0:T(8,128)} custom-call(s32[14]{0:T(128)} %stack.140.where, f32[128,1280]{1,0:T(8,128)} %copy-done.1, f32[128,1280]{1,0:T(8,128)} %copy-done.7, f32[96,1280]{1,0:T(8,128)} %collective-permute-done.40.refs_2_, f32[96,1280]{1,0:T(8,128)} %copy-done.8, ...), custom_call_target="tpu_custom_call", output_to_operand_aliasing={{}: (9, {})} | custom-call | tf_op jit(solution)/shard_map/pallas_call | solution.py:175
  (140 shorter events, 63.5 us)
Async XLA Ops:
  10.0 10.3 %collective-permute-start.2 = (f32[64,1280]{1,0:T(8,128)S(1)}, f32[64,1280]{1,0:T(8,128)S(1)}, u32[]{:S(2)}, u32[]{:S(2)}) collective-permute-start(f32[64,1280]{1,0:T(8,128)S(1)} %get-tuple-element.35), channel_id=1, source_target_pairs={{0,32},{16,48},{32,64},{48,80},{64,96},{80,112},{96,0},{112,16},{1... | collective-permute-start | bytes 983048 | tf_op jit(solution)/shard_map/ppermute | solution.py:36
  10.0 10.3 %collective-permute-start.3 = (f32[64,1280]{1,0:T(8,128)S(1)}, f32[64,1280]{1,0:T(8,128)S(1)}, u32[]{:S(2)}, u32[]{:S(2)}) collective-permute-start(f32[64,1280]{1,0:T(8,128)S(1)} %get-tuple-element.36), channel_id=1, source_target_pairs={{0,96},{16,112},{32,0},{48,16},{64,32},{80,48},{96,64},{112,80},{1... | collective-permute-start | bytes 983048 | tf_op jit(solution)/shard_map/ppermute | solution.py:36
  23.9 17.4 %collective-permute-start.10 = (f32[128,1280]{1,0:T(8,128)S(1)}, f32[128,1280]{1,0:T(8,128)S(1)}, u32[]{:S(2)}, u32[]{:S(2)}) collective-permute-start(f32[128,1280]{1,0:T(8,128)S(1)} %get-tuple-element.38), channel_id=1, source_target_pairs={{0,32},{16,48},{32,64},{48,80},{64,96},{80,112},{96,0},{112,16},{1... | collective-permute-start | bytes 1966088 | tf_op jit(solution)/shard_map/ppermute | solution.py:36
  23.9 18.4 %collective-permute-start.9 = (f32[128,1280]{1,0:T(8,128)S(1)}, f32[128,1280]{1,0:T(8,128)S(1)}, u32[]{:S(2)}, u32[]{:S(2)}) collective-permute-start(f32[128,1280]{1,0:T(8,128)S(1)} %get-tuple-element.39), channel_id=1, source_target_pairs={{0,96},{16,112},{32,0},{48,16},{64,32},{80,48},{96,64},{112,80},{1... | collective-permute-start | bytes 1966088 | tf_op jit(solution)/shard_map/ppermute | solution.py:36
  28.8 13.5 %collective-permute-start.8 = (f32[2,1,1,1,1,64,1280]{6,5,4,3,2,1,0:T(8,128)S(1)}, f32[2,1,1,1,1,64,1280]{6,5,4,3,2,1,0:T(8,128)S(1)}, u32[]{:S(2)}, u32[]{:S(2)}) collective-permute-start(f32[2,1,1,1,1,64,1280]{6,5,4,3,2,1,0:T(8,128)S(1)} %get-tuple-element.80), channel_id=1, source_target_pairs={{0,16},{16,0},{32,48},{48,32},{64,80},{80,64},{96,112},{112,96},{1... | collective-permute-start | bytes 1966088 | tf_op jit(solution)/shard_map/ppermute | solution.py:36
  29.5 14.1 %collective-permute-start.5 = (f32[2,1,1,1,1,64,1280]{6,5,0,4,3,2,1:T(8,128)S(1)}, f32[2,1,1,1,1,64,1280]{6,5,0,4,3,2,1:T(8,128)S(1)}, u32[]{:S(2)}, u32[]{:S(2)}) collective-permute-start(f32[2,1,1,1,1,64,1280]{6,5,0,4,3,2,1:T(8,128)S(1)} %get-tuple-element.81), channel_id=1, source_target_pairs={{0,16},{16,0},{32,48},{48,32},{64,80},{80,64},{96,112},{112,96},{1... | collective-permute-start | bytes 1966088 | tf_op jit(solution)/shard_map/ppermute | solution.py:36
  29.6 14.0 %collective-permute-start.4 = (f32[2,1,1,1,1,64,1280]{6,5,0,4,3,2,1:T(8,128)S(1)}, f32[2,1,1,1,1,64,1280]{6,5,0,4,3,2,1:T(8,128)S(1)}, u32[]{:S(2)}, u32[]{:S(2)}) collective-permute-start(f32[2,1,1,1,1,64,1280]{6,5,0,4,3,2,1:T(8,128)S(1)} %get-tuple-element.82), channel_id=1, source_target_pairs={{0,16},{16,0},{32,48},{48,32},{64,80},{80,64},{96,112},{112,96},{1... | collective-permute-start | bytes 1966088 | tf_op jit(solution)/shard_map/ppermute | solution.py:36
  45.8 17.9 %collective-permute-start.11 = (f32[2,64,1280]{2,1,0:T(8,128)S(1)}, f32[2,64,1280]{2,1,0:T(8,128)S(1)}, u32[]{:S(2)}, u32[]{:S(2)}) collective-permute-start(f32[2,64,1280]{2,1,0:T(8,128)S(1)} %get-tuple-element.45), channel_id=1, source_target_pairs={{0,32},{16,48},{32,64},{48,80},{64,96},{80,112},{96,0},{112,16},{1... | collective-permute-start | bytes 1966088 | tf_op jit(solution)/shard_map/ppermute | solution.py:36
  45.9 17.8 %collective-permute-start.12 = (f32[2,64,1280]{2,1,0:T(8,128)S(1)}, f32[2,64,1280]{2,1,0:T(8,128)S(1)}, u32[]{:S(2)}, u32[]{:S(2)}) collective-permute-start(f32[2,64,1280]{2,1,0:T(8,128)S(1)} %get-tuple-element.46), channel_id=1, source_target_pairs={{0,96},{16,112},{32,0},{48,16},{64,32},{80,48},{96,64},{112,80},{1... | collective-permute-start | bytes 1966088 | tf_op jit(solution)/shard_map/ppermute | solution.py:36
  48.5 27.8 %collective-permute-start.13 = (f32[2,64,1280]{2,1,0:T(8,128)S(1)}, f32[2,64,1280]{2,1,0:T(8,128)S(1)}, u32[]{:S(2)}, u32[]{:S(2)}) collective-permute-start(f32[2,64,1280]{2,1,0:T(8,128)S(1)} %get-tuple-element.47), channel_id=1, source_target_pairs={{0,64},{16,80},{32,96},{48,112},{64,0},{80,16},{96,32},{112,48},{1... | collective-permute-start | bytes 1966088 | tf_op jit(solution)/shard_map/ppermute | solution.py:36
  48.5 27.8 %collective-permute-start.14 = (f32[2,64,1280]{2,1,0:T(8,128)S(1)}, f32[2,64,1280]{2,1,0:T(8,128)S(1)}, u32[]{:S(2)}, u32[]{:S(2)}) collective-permute-start(f32[2,64,1280]{2,1,0:T(8,128)S(1)} %pad_maximum_fusion.4), channel_id=1, source_target_pairs={{0,128},{16,144},{32,160},{48,176},{64,192},{80,208},{96,224},{112... | collective-permute-start | bytes 1966088 | tf_op jit(solution)/shard_map/ppermute | solution.py:36
  123.0 23.4 %collective-permute-start.32 = (f32[2,64,1280]{2,1,0:T(8,128)S(1)}, f32[2,64,1280]{2,1,0:T(8,128)S(1)}, u32[]{:S(2)}, u32[]{:S(2)}) collective-permute-start(f32[2,64,1280]{2,1,0:T(8,128)S(1)} %multiply_subtract_fusion), channel_id=1, source_target_pairs={{0,16},{16,0},{32,48},{48,32},{64,80},{80,64},{96,112},{112,96},{1... | collective-permute-start | bytes 1966088 | tf_op jit(solution)/shard_map/ppermute | solution.py:36
  126.2 20.2 %collective-permute-start.30 = (f32[2,64,1280]{2,1,0:T(8,128)S(1)}, f32[2,64,1280]{2,1,0:T(8,128)S(1)}, u32[]{:S(2)}, u32[]{:S(2)}) collective-permute-start(f32[2,64,1280]{2,1,0:T(8,128)S(1)} %multiply_subtract_fusion), channel_id=1, source_target_pairs={{0,96},{16,112},{32,0},{48,16},{64,32},{80,48},{96,64},{112,80},{1... | collective-permute-start | bytes 1966088 | tf_op jit(solution)/shard_map/ppermute | solution.py:36
  126.6 20.7 %collective-permute-start.29 = (f32[2,64,1280]{2,1,0:T(8,128)S(1)}, f32[2,64,1280]{2,1,0:T(8,128)S(1)}, u32[]{:S(2)}, u32[]{:S(2)}) collective-permute-start(f32[2,64,1280]{2,1,0:T(8,128)S(1)} %multiply_subtract_fusion), channel_id=1, source_target_pairs={{0,32},{16,48},{32,64},{48,80},{64,96},{80,112},{96,0},{112,16},{1... | collective-permute-start | bytes 1966088 | tf_op jit(solution)/shard_map/ppermute | solution.py:36
  127.8 18.7 %collective-permute-start.31 = (f32[64,1280]{1,0:T(8,128)S(1)}, f32[64,1280]{1,0:T(8,128)S(1)}, u32[]{:S(2)}, u32[]{:S(2)}) collective-permute-start(f32[64,1280]{1,0:T(8,128)S(1)} %get-tuple-element.95), channel_id=1, source_target_pairs={{0,128},{16,144},{32,160},{48,176},{64,192},{80,208},{96,224},{112... | collective-permute-start | bytes 983048 | tf_op jit(solution)/shard_map/ppermute | solution.py:36
  147.4 19.5 %collective-permute-start.33 = (f32[128,1280]{1,0:T(8,128)S(1)}, f32[128,1280]{1,0:T(8,128)}, u32[]{:S(2)}, u32[]{:S(2)}) collective-permute-start(f32[128,1280]{1,0:T(8,128)S(1)} %get-tuple-element.53), channel_id=1, source_target_pairs={{0,32},{16,48},{32,64},{48,80},{64,96},{80,112},{96,0},{112,16},{1... | collective-permute-start | bytes 1966088 | tf_op jit(solution)/shard_map/ppermute | solution.py:36
  148.0 18.9 %collective-permute-start.34 = (f32[128,1280]{1,0:T(8,128)S(1)}, f32[128,1280]{1,0:T(8,128)}, u32[]{:S(2)}, u32[]{:S(2)}) collective-permute-start(f32[128,1280]{1,0:T(8,128)S(1)} %get-tuple-element.54), channel_id=1, source_target_pairs={{0,96},{16,112},{32,0},{48,16},{64,32},{80,48},{96,64},{112,80},{1... | collective-permute-start | bytes 1966088 | tf_op jit(solution)/shard_map/ppermute | solution.py:36
  150.4 16.5 %collective-permute-start.36 = (f32[2,64,1280]{2,1,0:T(8,128)S(1)}, f32[2,64,1280]{2,1,0:T(8,128)S(1)}, u32[]{:S(2)}, u32[]{:S(2)}) collective-permute-start(f32[2,64,1280]{2,1,0:T(8,128)S(1)} %collective-permute-done.29), channel_id=1, source_target_pairs={{0,16},{16,0},{32,48},{48,32},{64,80},{80,64},{96,112},{112,96},{1... | collective-permute-start | bytes 1966088 | tf_op jit(solution)/shard_map/ppermute | solution.py:36
  152.3 14.7 %collective-permute-start.37 = (f32[2,64,1280]{2,1,0:T(8,128)S(1)}, f32[2,64,1280]{2,1,0:T(8,128)}, u32[]{:S(2)}, u32[]{:S(2)}) collective-permute-start(f32[2,64,1280]{2,1,0:T(8,128)S(1)} %collective-permute-done.30), channel_id=1, source_target_pairs={{0,16},{16,0},{32,48},{48,32},{64,80},{80,64},{96,112},{112,96},{1... | collective-permute-start | bytes 1966088 | tf_op jit(solution)/shard_map/ppermute | solution.py:36
  152.3 14.6 %collective-permute-start.35 = (f32[64,1280]{1,0:T(8,128)S(1)}, f32[64,1280]{1,0:T(8,128)S(1)}, u32[]{:S(2)}, u32[]{:S(2)}) collective-permute-start(f32[64,1280]{1,0:T(8,128)S(1)} %get-tuple-element.94), channel_id=1, source_target_pairs={{0,128},{16,144},{32,160},{48,176},{64,192},{80,208},{96,224},{112... | collective-permute-start | bytes 983048 | tf_op jit(solution)/shard_map/ppermute | solution.py:36
  168.1 9.1 %collective-permute-start.38 = (f32[128,1280]{1,0:T(8,128)}, f32[128,1280]{1,0:T(8,128)}, u32[]{:S(2)}, u32[]{:S(2)}) collective-permute-start(f32[128,1280]{1,0:T(8,128)} %collective-permute-done.33.refs_6_), channel_id=1, source_target_pairs={{0,16},{16,0},{32,48},{48,32},{64,80},{80,64},{96,112},{112,96},{1... | collective-permute-start | bytes 1966088 | tf_op jit(solution)/shard_map/ppermute | solution.py:36
  173.8 20.8 %collective-permute-start.40 = (f32[96,1280]{1,0:T(8,128)}, f32[96,1280]{1,0:T(8,128)}, u32[]{:S(2)}, u32[]{:S(2)}) collective-permute-start(f32[96,1280]{1,0:T(8,128)} %get-tuple-element.60), channel_id=1, source_target_pairs={{0,32},{16,48},{32,64},{48,80},{64,96},{80,112},{96,0},{112,16},{1... | collective-permute-start | bytes 1474568 | tf_op jit(solution)/shard_map/ppermute | solution.py:36
  173.8 20.8 %collective-permute-start.41 = (f32[96,1280]{1,0:T(8,128)}, f32[96,1280]{1,0:T(8,128)}, u32[]{:S(2)}, u32[]{:S(2)}) collective-permute-start(f32[96,1280]{1,0:T(8,128)} %get-tuple-element.61), channel_id=1, source_target_pairs={{0,96},{16,112},{32,0},{48,16},{64,32},{80,48},{96,64},{112,80},{1... | collective-permute-start | bytes 1474568 | tf_op jit(solution)/shard_map/ppermute | solution.py:36
  176.5 17.1 %collective-permute-start.42 = (f32[64,1280]{1,0:T(8,128)S(1)}, f32[64,1280]{1,0:T(8,128)}, u32[]{:S(2)}, u32[]{:S(2)}) collective-permute-start(f32[64,1280]{1,0:T(8,128)S(1)} %collective-permute-done.35), channel_id=1, source_target_pairs={{0,64},{16,80},{32,96},{48,112},{64,0},{80,16},{96,32},{112,48},{1... | collective-permute-start | bytes 983048 | tf_op jit(solution)/shard_map/ppermute | solution.py:36
  (38 other events, 638.0 us)
where the time goes:
time: 209 us; the launch traced here: 206 us
  waiting for transfers between devices  88.2 us (42%)
  starting transfers between devices  84.5 us (40%)
  other arithmetic  11.5 us (6%)
  Pallas kernels  10.4 us (5%)
  local copies, waits for them, and re-layouts  10.2 us (5%)
    ppermute x35, waiting for transfers between devices, send(): return lax.ppermute(value, 'dp', perm)  80.2 us
    ppermute x35, starting transfers between devices, send(): return lax.ppermute(value, 'dp', perm)  61.6 us
    ppermute x12, starting transfers between devices, sum4(): second, third, fourth = (lax.ppermute(value, axis, perm) for perm in perms)  22.9 us
    pallas_call x2, Pallas kernels, put(): pl.pallas_call(functools.partial(place_kernel, slabs), out_shape=jax.Shap...  10.4 us
    ppermute x12, waiting for transfers between devices, sum4(): second, third, fourth = (lax.ppermute(value, axis, perm) for perm in perms)  8.01 us
  transfers between devices with their start and end apart: 47, of which 18 were waited for; matrix products, arithmetic and copies ran while one was open for 4% of the time, Pallas kernels for 3%

commit v1 on v0

--- a/solution.py
+++ b/solution.py
@@ -188,24 +188,25 @@
 
 def gather_rows(shard):
     zh, x, c = place()
-    half = ROWS // 2
-
-    def row(dc, expert, dz, dx, first=0):
+
+    def row(dc, expert, dz, dx):
         at_c = (zh + dz) % 2 * 8 + (x + dx) % 4 * 2 + (c + dc) % 2
-        return expert * 1024 + ROWS * at_c + first
+        return expert * 1024 + ROWS * at_c
 
     def write(out, pieces):
         arrays, slabs, rows = [], [], []
         for mine, theirs, parts in pieces:
             for dc, array in enumerate((mine, theirs)):
-                start = 0
-                for size, *to in parts:
-                    slabs.append((len(arrays), start, size))
+                for i, to in enumerate(parts):
+                    slabs.append((len(arrays), i * ROWS, ROWS))
                     rows.append(row(dc, *to))
-                    start += size
                 arrays.append(array)
         return put(out, arrays, slabs, rows)
 
+    def with_partner(array, parts):
+        return array, send(array, CORE), parts
+
+    both = lambda dz, dx: [(e, dz, dx) for e in range(E)]
     other = [send(shard[e], ZHALF) for e in range(E)]
     left, right = send(shard, PLUS), send(shard, MINUS)
     shard_c = send(shard, CORE)
@@ -214,41 +215,35 @@
     plus = jnp.concatenate([left[0], other_0])
     minus = jnp.concatenate([right[1], other_0])
     plus, minus = lax.optimization_barrier((plus, minus))
-    from_left, from_right = send(plus, PLUS), send(minus, MINUS)
-    left_c, right_c = send(left, CORE), send(right, CORE)
-
-    from_left, from_right, other_1, left_c, right_c = lax.optimization_barrier(
-        (from_left, from_right, other[1], left_c, right_c)
-    )
-    plus = jnp.concatenate([other_1, from_left[ROWS : ROWS + half]])
-    minus = jnp.concatenate([other_1, from_right[ROWS + half :]])
-    plus, minus = lax.optimization_barrier((plus, minus))
-    last_left, last_right = send(plus, PLUS), send(minus, MINUS)
-    far_1 = send(other_1, FAR)
-    from_left_c, from_right_c = send(from_left, CORE), send(from_right, CORE)
+    from_left, from_right, far_0 = send(plus, PLUS), send(minus, MINUS), send(other_0, FAR)
+
+    from_left, from_right, far_0, other_1 = lax.optimization_barrier(
+        (from_left, from_right, far_0, other[1])
+    )
+    left_1, right_1, far_1 = send(other_1, PLUS), send(other_1, MINUS), send(other_1, FAR)
     others = jnp.concatenate([other_0, other_1])
-    both = lambda dz, dx: [(ROWS, e, dz, dx) for e in range(E)]
     out = write(
         None,
         [
             (shard, shard_c, both(0, 0)),
-            (left, left_c, both(0, 3)),
-            (right, right_c, both(0, 1)),
-            (from_left, from_left_c, [(ROWS, 0, 0, 2), (ROWS, 0, 1, 3)]),
-            (from_right, from_right_c, [(ROWS, 1, 0, 2), (ROWS, 0, 1, 1)]),
+            with_partner(left, both(0, 3)),
+            with_partner(right, both(0, 1)),
+            with_partner(from_left, [(0, 0, 2), (0, 1, 3)]),
+            with_partner(from_right, [(1, 0, 2), (0, 1, 1)]),
+            with_partner(others, both(1, 0)),
         ],
     )
 
-    out, last_left, last_right, far_1, others = lax.optimization_barrier(
-        (out, last_left, last_right, far_1, others)
+    out, left_1, right_1, far_1, far_0 = lax.optimization_barrier(
+        (out, left_1, right_1, far_1, far_0)
     )
     return write(
         out,
         [
-            (others, send(others, CORE), both(1, 0)),
-            (last_left, send(last_left, CORE), [(ROWS, 1, 1, 3), (half, 0, 1, 2, 0)]),
-            (last_right, send(last_right, CORE), [(ROWS, 1, 1, 1), (half, 0, 1, 2, half)]),
-            (far_1, send(far_1, CORE), [(ROWS, 1, 1, 2)]),
+            with_partner(left_1, [(1, 1, 3)]),
+            with_partner(right_1, [(1, 1, 1)]),
+            with_partner(far_1, [(1, 1, 2)]),
+            with_partner(far_0, [(0, 1, 2)]),
         ],
     )
 

time: 209 us -> 202 us (0.967); the launches traced: 206 us -> 201 us
  waiting for transfers between devices: 88.2 us -> 80.6 us
  starting transfers between devices: 84.5 us -> 89.6 us
    ppermute x35 -> x37, waiting for transfers between devices: 80.2 us -> 72.6 us  [send(): return lax.ppermute(value, 'dp', perm)]
    ppermute x35 -> x37, starting transfers between devices: 61.6 us -> 66.7 us  [send(): return lax.ppermute(value, 'dp', perm)]
  transfers between devices with their start and end apart: 47 -> 49, of which waited for: 18 -> 22; matrix products, arithmetic and copies ran while one was open for 4% -> 4% of each run, Pallas kernels for 3% -> 3%
where the time goes in v1:
time: 202 us; the launch traced here: 201 us
  starting transfers between devices  89.6 us (44%)
  waiting for transfers between devices  80.6 us (40%)
  other arithmetic  10.5 us (5%)
  Pallas kernels  10.3 us (5%)
  local copies, waits for them, and re-layouts  8.98 us (4%)
    ppermute x37, waiting for transfers between devices, send(): return lax.ppermute(value, 'dp', perm)  72.6 us
    ppermute x37, starting transfers between devices, send(): return lax.ppermute(value, 'dp', perm)  66.7 us
    ppermute x12, starting transfers between devices, sum4(): second, third, fourth = (lax.ppermute(value, axis, perm) for perm in perms)  22.9 us
    pallas_call x2, Pallas kernels, put(): pl.pallas_call(functools.partial(place_kernel, slabs), out_shape=jax.Shap...  10.3 us
    ppermute x12, waiting for transfers between devices, sum4(): second, third, fourth = (lax.ppermute(value, axis, perm) for perm in perms)  8.01 us
  transfers between devices with their start and end apart: 49, of which 22 were waited for; matrix products, arithmetic and copies ran while one was open for 4% of the time, Pallas kernels for 3%

profile of v1, /device:TPU:1, one launch (start us, length us, event | category | flops | bytes accessed | tf_op | source)
XLA Modules:
  0.0 201.2 jit_solution(1003999594582266225)
XLA Ops:
  1.9 3.3 %collective-permute-start = (f32[2,1,1,1,1,64,1280]{6,5,4,3,2,1,0:T(8,128)S(1)}, f32[2,1,1,1,1,64,1280]{6,5,4,3,2,1,0:T(8,128)S(1)}, u32[]{:S(2)}, u32[]{:S(2)}) collective-permute-start(f32[2,1,1,1,1,64,1280]{6,5,4,3,2,1,0:T(8,128)S(1)} %constant_dynamic-slice_fusion.3), channel_id=1, source_target_pairs={{0,16},{16,0},{32,48},{48,32},{64,80},{80,64},{96,112},{112,96},{1... | collective-permute-start | bytes 1966088 | tf_op jit(solution)/shard_map/ppermute | solution.py:36
  13.9 6.3 %collective-permute-done.2 = f32[64,1280]{1,0:T(8,128)S(1)} collective-permute-done((f32[64,1280]{1,0:T(8,128)S(1)}, f32[64,1280]{1,0:T(8,128)S(1)}, u32[]{:S(2)}, u32[]{:S(2)}) %collective-permute-start.2) | collective-permute-done | bytes 327712 | tf_op jit(solution)/shard_map/ppermute | solution.py:36
  23.9 2.8 %collective-permute-start.9 = (f32[128,1280]{1,0:T(8,128)S(1)}, f32[128,1280]{1,0:T(8,128)S(1)}, u32[]{:S(2)}, u32[]{:S(2)}) collective-permute-start(f32[128,1280]{1,0:T(8,128)S(1)} %get-tuple-element.36), channel_id=1, source_target_pairs={{0,96},{16,112},{32,0},{48,16},{64,32},{80,48},{96,64},{112,80},{1... | collective-permute-start | bytes 1966088 | tf_op jit(solution)/shard_map/ppermute | solution.py:36
  30.0 11.3 %collective-permute-done.10 = f32[128,1280]{1,0:T(8,128)S(1)} collective-permute-done((f32[128,1280]{1,0:T(8,128)S(1)}, f32[128,1280]{1,0:T(8,128)S(1)}, u32[]{:S(2)}, u32[]{:S(2)}) %collective-permute-start.10) | collective-permute-done | bytes 655392 | tf_op jit(solution)/shard_map/ppermute | solution.py:36
  48.5 5.2 %collective-permute-start.14 = (f32[2,64,1280]{2,1,0:T(8,128)S(1)}, f32[2,64,1280]{2,1,0:T(8,128)S(1)}, u32[]{:S(2)}, u32[]{:S(2)}) collective-permute-start(f32[2,64,1280]{2,1,0:T(8,128)S(1)} %pad_maximum_fusion.4), channel_id=1, source_target_pairs={{0,128},{16,144},{32,160},{48,176},{64,192},{80,208},{96,224},{112... | collective-permute-start | bytes 1966088 | tf_op jit(solution)/shard_map/ppermute | solution.py:36
  53.7 10.0 %collective-permute-done.11 = f32[2,64,1280]{2,1,0:T(8,128)S(1)} collective-permute-done((f32[2,64,1280]{2,1,0:T(8,128)S(1)}, f32[2,64,1280]{2,1,0:T(8,128)S(1)}, u32[]{:S(2)}, u32[]{:S(2)}) %collective-permute-start.11) | collective-permute-done | bytes 655392 | tf_op jit(solution)/shard_map/ppermute | solution.py:36
  63.7 12.7 %collective-permute-done.13 = f32[2,64,1280]{2,1,0:T(8,128)S(1)} collective-permute-done((f32[2,64,1280]{2,1,0:T(8,128)S(1)}, f32[2,64,1280]{2,1,0:T(8,128)S(1)}, u32[]{:S(2)}, u32[]{:S(2)}) %collective-permute-start.13) | collective-permute-done | bytes 655392 | tf_op jit(solution)/shard_map/ppermute | solution.py:36
  76.7 2.8 %collective-permute-start.17 = (f32[2,64]{1,0:T(2,128)S(1)}, f32[2,64]{1,0:T(2,128)S(1)}, u32[]{:S(2)}, u32[]{:S(2)}) collective-permute-start(f32[2,64]{1,0:T(2,128)S(1)} %get-tuple-element.68), channel_id=1, source_target_pairs={{0,3},{1,0},{2,1},{3,2},{4,7},{5,4},{6,5},{7,6},{8,11},{9,8},{10,9... | collective-permute-start | bytes 1544 | tf_op jit(solution)/shard_map/ppermute | solution.py:40
  79.5 2.8 %collective-permute-start.16 = (f32[2,64]{1,0:T(2,128)S(1)}, f32[2,64]{1,0:T(2,128)S(1)}, u32[]{:S(2)}, u32[]{:S(2)}) collective-permute-start(f32[2,64]{1,0:T(2,128)S(1)} %get-tuple-element.68), channel_id=1, source_target_pairs={{0,1},{1,2},{2,3},{3,0},{4,5},{5,6},{6,7},{7,4},{8,9},{9,10},{10,1... | collective-permute-start | bytes 1544 | tf_op jit(solution)/shard_map/ppermute | solution.py:40
  82.3 3.3 %collective-permute-start.15 = (f32[2,64]{1,0:T(2,128)S(1)}, f32[2,64]{1,0:T(2,128)S(1)}, u32[]{:S(2)}, u32[]{:S(2)}) collective-permute-start(f32[2,64]{1,0:T(2,128)S(1)} %get-tuple-element.68), channel_id=1, source_target_pairs={{0,2},{1,3},{2,0},{3,1},{4,6},{5,7},{6,4},{7,5},{8,10},{9,11},{10,... | collective-permute-start | bytes 1544 | tf_op jit(solution)/shard_map/ppermute | solution.py:40
  94.2 2.9 %collective-permute-start.23 = (f32[8,1280]{1,0:T(8,128)S(1)}, f32[8,1280]{1,0:T(8,128)S(1)}, u32[]{:S(2)}, u32[]{:S(2)}) collective-permute-start(f32[8,1280]{1,0:T(8,128)S(1)} %add_add_fusion.2), channel_id=1, source_target_pairs={{0,12},{4,0},{8,4},{12,8},{1,13},{5,1},{9,5},{13,9},{2,14},{6,2},{... | collective-permute-start | bytes 122888 | tf_op jit(solution)/shard_map/ppermute | solution.py:40
  98.8 2.9 %collective-permute-done.22 = f32[8,1280]{1,0:T(8,128)S(1)} collective-permute-done((f32[8,1280]{1,0:T(8,128)S(1)}, f32[8,1280]{1,0:T(8,128)S(1)}, u32[]{:S(2)}, u32[]{:S(2)}) %collective-permute-start.22) | collective-permute-done | bytes 40992 | tf_op jit(solution)/shard_map/ppermute | solution.py:40
  101.6 6.3 %collective-permute-start.24 = (f32[8,1280]{1,0:T(8,128)S(1)}, f32[8,1280]{1,0:T(8,128)S(1)}, u32[]{:S(2)}, u32[]{:S(2)}) collective-permute-start(f32[8,1280]{1,0:T(8,128)S(1)} %add_add_fusion.1), channel_id=1, source_target_pairs={{0,16},{16,0},{32,48},{48,32},{64,80},{80,64},{96,112},{112,96},{1... | collective-permute-start | bytes 122888 | tf_op jit(solution)/shard_map/ppermute | solution.py:36
  108.8 5.6 %collective-permute-start.25 = (f32[8,1280]{1,0:T(8,128)S(1)}, f32[8,1280]{1,0:T(8,128)S(1)}, u32[]{:S(2)}, u32[]{:S(2)}) collective-permute-start(f32[8,1280]{1,0:T(8,128)S(1)} %add.790), channel_id=1, source_target_pairs={{0,128},{16,144},{32,160},{48,176},{64,192},{80,208},{96,224},{112... | collective-permute-start | bytes 122888 | tf_op jit(solution)/shard_map/ppermute | solution.py:36
  123.1 3.2 %collective-permute-start.32 = (f32[2,64,1280]{2,1,0:T(8,128)S(1)}, f32[2,64,1280]{2,1,0:T(8,128)S(1)}, u32[]{:S(2)}, u32[]{:S(2)}) collective-permute-start(f32[2,64,1280]{2,1,0:T(8,128)S(1)} %multiply_subtract_fusion), channel_id=1, source_target_pairs={{0,16},{16,0},{32,48},{48,32},{64,80},{80,64},{96,112},{112,96},{1... | collective-permute-start | bytes 1966088 | tf_op jit(solution)/shard_map/ppermute | solution.py:36
  127.8 6.2 %collective-permute-start.31 = (f32[64,1280]{1,0:T(8,128)S(1)}, f32[64,1280]{1,0:T(8,128)S(1)}, u32[]{:S(2)}, u32[]{:S(2)}) collective-permute-start(f32[64,1280]{1,0:T(8,128)S(1)} %get-tuple-element.89), channel_id=1, source_target_pairs={{0,128},{16,144},{32,160},{48,176},{64,192},{80,208},{96,224},{112... | collective-permute-start | bytes 983048 | tf_op jit(solution)/shard_map/ppermute | solution.py:36
  134.0 12.5 %collective-permute-done.31 = f32[64,1280]{1,0:T(8,128)S(1)} collective-permute-done((f32[64,1280]{1,0:T(8,128)S(1)}, f32[64,1280]{1,0:T(8,128)S(1)}, u32[]{:S(2)}, u32[]{:S(2)}) %collective-permute-start.31) | collective-permute-done | bytes 327712 | tf_op jit(solution)/shard_map/ppermute | solution.py:36
  149.7 5.1 %collective-permute-start.38 = (f32[64,1280]{1,0:T(8,128)S(1)}, f32[64,1280]{1,0:T(8,128)}, u32[]{:S(2)}, u32[]{:S(2)}) collective-permute-start(f32[64,1280]{1,0:T(8,128)S(1)} %get-tuple-element.88), channel_id=1, source_target_pairs={{0,128},{16,144},{32,160},{48,176},{64,192},{80,208},{96,224},{112... | collective-permute-start | bytes 983048 | tf_op jit(solution)/shard_map/ppermute | solution.py:36
  157.9 5.1 %collective-permute-done.38 = f32[64,1280]{1,0:T(8,128)} collective-permute-done((f32[64,1280]{1,0:T(8,128)S(1)}, f32[64,1280]{1,0:T(8,128)}, u32[]{:S(2)}, u32[]{:S(2)}) %collective-permute-start.38) | collective-permute-done | bytes 327712 | tf_op jit(solution)/shard_map/ppermute | solution.py:36
  163.0 5.0 %collective-permute-start.34 = (f32[2,64,1280]{2,1,0:T(8,128)S(1)}, f32[2,64,1280]{2,1,0:T(8,128)S(1)}, u32[]{:S(2)}, u32[]{:S(2)}) collective-permute-start(f32[2,64,1280]{2,1,0:T(8,128)S(1)} %collective-permute-done.30), channel_id=1, source_target_pairs={{0,16},{16,0},{32,48},{48,32},{64,80},{80,64},{96,112},{112,96},{1... | collective-permute-start | bytes 1966088 | tf_op jit(solution)/shard_map/ppermute | solution.py:36
  175.4 2.8 %collective-permute-start.43 = (f32[64,1280]{1,0:T(8,128)}, f32[64,1280]{1,0:T(8,128)}, u32[]{:S(2)}, u32[]{:S(2)}) collective-permute-start(f32[64,1280]{1,0:T(8,128)} %collective-permute-done.38), channel_id=1, source_target_pairs={{0,96},{16,112},{32,0},{48,16},{64,32},{80,48},{96,64},{112,80},{1... | collective-permute-start | bytes 983048 | tf_op jit(solution)/shard_map/ppermute | solution.py:36
  179.9 7.0 %shard_map.67.refs_8_ = f32[2048,1280]{1,0:T(8,128)} custom-call(s32[24]{0:T(128)} %stack.153.where, f32[128,1280]{1,0:T(8,128)} %bitcast.120, f32[128,1280]{1,0:T(8,128)} %bitcast.123, f32[128,1280]{1,0:T(8,128)} %bitcast.122, f32[128,1280]{1,0:T(8,128)} %bitcast.124, f32[128,1280]{1,0:T(8,128)} %bitcast.121, f32[128,1280]{1,0:T(8,128)} %bitcast.125, ...), custom_call_target="tpu_custom_call" | custom-call | tf_op jit(solution)/shard_map/pallas_call | solution.py:175
  187.0 5.6 %collective-permute-done.43.refs_2_ = f32[64,1280]{1,0:T(8,128)} collective-permute-done((f32[64,1280]{1,0:T(8,128)}, f32[64,1280]{1,0:T(8,128)}, u32[]{:S(2)}, u32[]{:S(2)}) %collective-permute-start.43) | collective-permute-done | bytes 327712 | tf_op jit(solution)/shard_map/ppermute | solution.py:36
  197.8 3.3 %shard_map.68 = f32[2048,1280]{1,0:T(8,128)} custom-call(s32[8]{0:T(128)} %stack.128.where, f32[64,1280]{1,0:T(8,128)} %collective-permute-done.42.refs_0_, f32[64,1280]{1,0:T(8,128)} %copy-done.11, f32[64,1280]{1,0:T(8,128)} %collective-permute-done.43.refs_2_, f32[64,1280]{1,0:T(8,128)} %copy-done.12, ...), custom_call_target="tpu_custom_call", output_to_operand_aliasing={{}: (9, {})} | custom-call | tf_op jit(solution)/shard_map/pallas_call | solution.py:175
  (150 shorter events, 66.3 us)
Async XLA Ops:
  10.0 10.3 %collective-permute-start.2 = (f32[64,1280]{1,0:T(8,128)S(1)}, f32[64,1280]{1,0:T(8,128)S(1)}, u32[]{:S(2)}, u32[]{:S(2)}) collective-permute-start(f32[64,1280]{1,0:T(8,128)S(1)} %get-tuple-element.32), channel_id=1, source_target_pairs={{0,32},{16,48},{32,64},{48,80},{64,96},{80,112},{96,0},{112,16},{1... | collective-permute-start | bytes 983048 | tf_op jit(solution)/shard_map/ppermute | solution.py:36
  10.0 10.3 %collective-permute-start.3 = (f32[64,1280]{1,0:T(8,128)S(1)}, f32[64,1280]{1,0:T(8,128)S(1)}, u32[]{:S(2)}, u32[]{:S(2)}) collective-permute-start(f32[64,1280]{1,0:T(8,128)S(1)} %get-tuple-element.33), channel_id=1, source_target_pairs={{0,96},{16,112},{32,0},{48,16},{64,32},{80,48},{96,64},{112,80},{1... | collective-permute-start | bytes 983048 | tf_op jit(solution)/shard_map/ppermute | solution.py:36
  23.9 17.4 %collective-permute-start.10 = (f32[128,1280]{1,0:T(8,128)S(1)}, f32[128,1280]{1,0:T(8,128)S(1)}, u32[]{:S(2)}, u32[]{:S(2)}) collective-permute-start(f32[128,1280]{1,0:T(8,128)S(1)} %get-tuple-element.35), channel_id=1, source_target_pairs={{0,32},{16,48},{32,64},{48,80},{64,96},{80,112},{96,0},{112,16},{1... | collective-permute-start | bytes 1966088 | tf_op jit(solution)/shard_map/ppermute | solution.py:36
  23.9 18.4 %collective-permute-start.9 = (f32[128,1280]{1,0:T(8,128)S(1)}, f32[128,1280]{1,0:T(8,128)S(1)}, u32[]{:S(2)}, u32[]{:S(2)}) collective-permute-start(f32[128,1280]{1,0:T(8,128)S(1)} %get-tuple-element.36), channel_id=1, source_target_pairs={{0,96},{16,112},{32,0},{48,16},{64,32},{80,48},{96,64},{112,80},{1... | collective-permute-start | bytes 1966088 | tf_op jit(solution)/shard_map/ppermute | solution.py:36
  28.8 13.5 %collective-permute-start.8 = (f32[2,1,1,1,1,64,1280]{6,5,4,3,2,1,0:T(8,128)S(1)}, f32[2,1,1,1,1,64,1280]{6,5,4,3,2,1,0:T(8,128)S(1)}, u32[]{:S(2)}, u32[]{:S(2)}) collective-permute-start(f32[2,1,1,1,1,64,1280]{6,5,4,3,2,1,0:T(8,128)S(1)} %get-tuple-element.74), channel_id=1, source_target_pairs={{0,16},{16,0},{32,48},{48,32},{64,80},{80,64},{96,112},{112,96},{1... | collective-permute-start | bytes 1966088 | tf_op jit(solution)/shard_map/ppermute | solution.py:36
  29.5 14.1 %collective-permute-start.5 = (f32[2,1,1,1,1,64,1280]{6,5,0,4,3,2,1:T(8,128)S(1)}, f32[2,1,1,1,1,64,1280]{6,5,0,4,3,2,1:T(8,128)S(1)}, u32[]{:S(2)}, u32[]{:S(2)}) collective-permute-start(f32[2,1,1,1,1,64,1280]{6,5,0,4,3,2,1:T(8,128)S(1)} %get-tuple-element.75), channel_id=1, source_target_pairs={{0,16},{16,0},{32,48},{48,32},{64,80},{80,64},{96,112},{112,96},{1... | collective-permute-start | bytes 1966088 | tf_op jit(solution)/shard_map/ppermute | solution.py:36
  29.6 14.0 %collective-permute-start.4 = (f32[2,1,1,1,1,64,1280]{6,5,0,4,3,2,1:T(8,128)S(1)}, f32[2,1,1,1,1,64,1280]{6,5,0,4,3,2,1:T(8,128)S(1)}, u32[]{:S(2)}, u32[]{:S(2)}) collective-permute-start(f32[2,1,1,1,1,64,1280]{6,5,0,4,3,2,1:T(8,128)S(1)} %get-tuple-element.76), channel_id=1, source_target_pairs={{0,16},{16,0},{32,48},{48,32},{64,80},{80,64},{96,112},{112,96},{1... | collective-permute-start | bytes 1966088 | tf_op jit(solution)/shard_map/ppermute | solution.py:36
  45.7 17.9 %collective-permute-start.11 = (f32[2,64,1280]{2,1,0:T(8,128)S(1)}, f32[2,64,1280]{2,1,0:T(8,128)S(1)}, u32[]{:S(2)}, u32[]{:S(2)}) collective-permute-start(f32[2,64,1280]{2,1,0:T(8,128)S(1)} %get-tuple-element.42), channel_id=1, source_target_pairs={{0,32},{16,48},{32,64},{48,80},{64,96},{80,112},{96,0},{112,16},{1... | collective-permute-start | bytes 1966088 | tf_op jit(solution)/shard_map/ppermute | solution.py:36
  45.8 17.8 %collective-permute-start.12 = (f32[2,64,1280]{2,1,0:T(8,128)S(1)}, f32[2,64,1280]{2,1,0:T(8,128)S(1)}, u32[]{:S(2)}, u32[]{:S(2)}) collective-permute-start(f32[2,64,1280]{2,1,0:T(8,128)S(1)} %get-tuple-element.43), channel_id=1, source_target_pairs={{0,96},{16,112},{32,0},{48,16},{64,32},{80,48},{96,64},{112,80},{1... | collective-permute-start | bytes 1966088 | tf_op jit(solution)/shard_map/ppermute | solution.py:36
  48.5 27.8 %collective-permute-start.13 = (f32[2,64,1280]{2,1,0:T(8,128)S(1)}, f32[2,64,1280]{2,1,0:T(8,128)S(1)}, u32[]{:S(2)}, u32[]{:S(2)}) collective-permute-start(f32[2,64,1280]{2,1,0:T(8,128)S(1)} %get-tuple-element.44), channel_id=1, source_target_pairs={{0,64},{16,80},{32,96},{48,112},{64,0},{80,16},{96,32},{112,48},{1... | collective-permute-start | bytes 1966088 | tf_op jit(solution)/shard_map/ppermute | solution.py:36
  48.5 27.8 %collective-permute-start.14 = (f32[2,64,1280]{2,1,0:T(8,128)S(1)}, f32[2,64,1280]{2,1,0:T(8,128)S(1)}, u32[]{:S(2)}, u32[]{:S(2)}) collective-permute-start(f32[2,64,1280]{2,1,0:T(8,128)S(1)} %pad_maximum_fusion.4), channel_id=1, source_target_pairs={{0,128},{16,144},{32,160},{48,176},{64,192},{80,208},{96,224},{112... | collective-permute-start | bytes 1966088 | tf_op jit(solution)/shard_map/ppermute | solution.py:36
  123.1 23.4 %collective-permute-start.32 = (f32[2,64,1280]{2,1,0:T(8,128)S(1)}, f32[2,64,1280]{2,1,0:T(8,128)S(1)}, u32[]{:S(2)}, u32[]{:S(2)}) collective-permute-start(f32[2,64,1280]{2,1,0:T(8,128)S(1)} %multiply_subtract_fusion), channel_id=1, source_target_pairs={{0,16},{16,0},{32,48},{48,32},{64,80},{80,64},{96,112},{112,96},{1... | collective-permute-start | bytes 1966088 | tf_op jit(solution)/shard_map/ppermute | solution.py:36
  126.3 20.2 %collective-permute-start.30 = (f32[2,64,1280]{2,1,0:T(8,128)S(1)}, f32[2,64,1280]{2,1,0:T(8,128)S(1)}, u32[]{:S(2)}, u32[]{:S(2)}) collective-permute-start(f32[2,64,1280]{2,1,0:T(8,128)S(1)} %multiply_subtract_fusion), channel_id=1, source_target_pairs={{0,96},{16,112},{32,0},{48,16},{64,32},{80,48},{96,64},{112,80},{1... | collective-permute-start | bytes 1966088 | tf_op jit(solution)/shard_map/ppermute | solution.py:36
  126.7 19.8 %collective-permute-start.29 = (f32[2,64,1280]{2,1,0:T(8,128)S(1)}, f32[2,64,1280]{2,1,0:T(8,128)S(1)}, u32[]{:S(2)}, u32[]{:S(2)}) collective-permute-start(f32[2,64,1280]{2,1,0:T(8,128)S(1)} %multiply_subtract_fusion), channel_id=1, source_target_pairs={{0,32},{16,48},{32,64},{48,80},{64,96},{80,112},{96,0},{112,16},{1... | collective-permute-start | bytes 1966088 | tf_op jit(solution)/shard_map/ppermute | solution.py:36
  127.8 18.7 %collective-permute-start.31 = (f32[64,1280]{1,0:T(8,128)S(1)}, f32[64,1280]{1,0:T(8,128)S(1)}, u32[]{:S(2)}, u32[]{:S(2)}) collective-permute-start(f32[64,1280]{1,0:T(8,128)S(1)} %get-tuple-element.89), channel_id=1, source_target_pairs={{0,128},{16,144},{32,160},{48,176},{64,192},{80,208},{96,224},{112... | collective-permute-start | bytes 983048 | tf_op jit(solution)/shard_map/ppermute | solution.py:36
  146.7 23.5 %collective-permute-start.35 = (f32[128,1280]{1,0:T(8,128)S(1)}, f32[128,1280]{1,0:T(8,128)S(1)}, u32[]{:S(2)}, u32[]{:S(2)}) collective-permute-start(f32[128,1280]{1,0:T(8,128)S(1)} %get-tuple-element.50), channel_id=1, source_target_pairs={{0,32},{16,48},{32,64},{48,80},{64,96},{80,112},{96,0},{112,16},{1... | collective-permute-start | bytes 1966088 | tf_op jit(solution)/shard_map/ppermute | solution.py:36
  147.3 23.7 %collective-permute-start.36 = (f32[128,1280]{1,0:T(8,128)S(1)}, f32[128,1280]{1,0:T(8,128)}, u32[]{:S(2)}, u32[]{:S(2)}) collective-permute-start(f32[128,1280]{1,0:T(8,128)S(1)} %get-tuple-element.51), channel_id=1, source_target_pairs={{0,96},{16,112},{32,0},{48,16},{64,32},{80,48},{96,64},{112,80},{1... | collective-permute-start | bytes 1966088 | tf_op jit(solution)/shard_map/ppermute | solution.py:36
  149.7 13.3 %collective-permute-start.38 = (f32[64,1280]{1,0:T(8,128)S(1)}, f32[64,1280]{1,0:T(8,128)}, u32[]{:S(2)}, u32[]{:S(2)}) collective-permute-start(f32[64,1280]{1,0:T(8,128)S(1)} %get-tuple-element.88), channel_id=1, source_target_pairs={{0,128},{16,144},{32,160},{48,176},{64,192},{80,208},{96,224},{112... | collective-permute-start | bytes 983048 | tf_op jit(solution)/shard_map/ppermute | solution.py:36
  154.7 15.5 %collective-permute-start.37 = (f32[64,1280]{1,0:T(8,128)S(1)}, f32[64,1280]{1,0:T(8,128)S(1)}, u32[]{:S(2)}, u32[]{:S(2)}) collective-permute-start(f32[64,1280]{1,0:T(8,128)S(1)} %collective-permute-done.31), channel_id=1, source_target_pairs={{0,64},{16,80},{32,96},{48,112},{64,0},{80,16},{96,32},{112,48},{1... | collective-permute-start | bytes 983048 | tf_op jit(solution)/shard_map/ppermute | solution.py:36
  155.2 19.7 %collective-permute-start.33 = (f32[2,64,1280]{2,1,0:T(8,128)S(1)}, f32[2,64,1280]{2,1,0:T(8,128)S(1)}, u32[]{:S(2)}, u32[]{:S(2)}) collective-permute-start(f32[2,64,1280]{2,1,0:T(8,128)S(1)} %collective-permute-done.29), channel_id=1, source_target_pairs={{0,16},{16,0},{32,48},{48,32},{64,80},{80,64},{96,112},{112,96},{1... | collective-permute-start | bytes 1966088 | tf_op jit(solution)/shard_map/ppermute | solution.py:36
  163.0 12.4 %collective-permute-start.34 = (f32[2,64,1280]{2,1,0:T(8,128)S(1)}, f32[2,64,1280]{2,1,0:T(8,128)S(1)}, u32[]{:S(2)}, u32[]{:S(2)}) collective-permute-start(f32[2,64,1280]{2,1,0:T(8,128)S(1)} %collective-permute-done.30), channel_id=1, source_target_pairs={{0,16},{16,0},{32,48},{48,32},{64,80},{80,64},{96,112},{112,96},{1... | collective-permute-start | bytes 1966088 | tf_op jit(solution)/shard_map/ppermute | solution.py:36
  174.9 12.1 %collective-permute-start.44 = (f32[64,1280]{1,0:T(8,128)}, f32[64,1280]{1,0:T(8,128)}, u32[]{:S(2)}, u32[]{:S(2)}) collective-permute-start(f32[64,1280]{1,0:T(8,128)} %collective-permute-done.38), channel_id=1, source_target_pairs={{0,64},{16,80},{32,96},{48,112},{64,0},{80,16},{96,32},{112,48},{1... | collective-permute-start | bytes 983048 | tf_op jit(solution)/shard_map/ppermute | solution.py:36
  175.4 17.1 %collective-permute-start.43 = (f32[64,1280]{1,0:T(8,128)}, f32[64,1280]{1,0:T(8,128)}, u32[]{:S(2)}, u32[]{:S(2)}) collective-permute-start(f32[64,1280]{1,0:T(8,128)} %collective-permute-done.38), channel_id=1, source_target_pairs={{0,96},{16,112},{32,0},{48,16},{64,32},{80,48},{96,64},{112,80},{1... | collective-permute-start | bytes 983048 | tf_op jit(solution)/shard_map/ppermute | solution.py:36
  179.2 14.2 %collective-permute-start.42 = (f32[64,1280]{1,0:T(8,128)}, f32[64,1280]{1,0:T(8,128)}, u32[]{:S(2)}, u32[]{:S(2)}) collective-permute-start(f32[64,1280]{1,0:T(8,128)} %collective-permute-done.38), channel_id=1, source_target_pairs={{0,32},{16,48},{32,64},{48,80},{64,96},{80,112},{96,0},{112,16},{1... | collective-permute-start | bytes 983048 | tf_op jit(solution)/shard_map/ppermute | solution.py:36
  (44 other events, 680.5 us)

commit v2 on v1

--- a/solution.py
+++ b/solution.py
@@ -108,10 +108,12 @@
         return (mine + theirs).reshape(E, ROWS, COLS)
 
     *terms, own = after([both_experts(dx) for dx in (1, 3, 2, 0)], rows)
-    *terms, away = lax.optimization_barrier((*terms, away))
+    terms[2] = [terms[2][e] for e in range(E)]
+    terms, away = lax.optimization_barrier((terms, away))
     other = send(away, ZHALF)
-    got = [send(term, perm) for term, perm in zip(terms, (PLUS, MINUS, FAR))]
-    return own + got[0] + got[1] + got[2] + other
+    left, right = send(terms[0], PLUS), send(terms[1], MINUS)
+    far = jnp.stack([send(terms[2][e], FAR) for e in range(E)])
+    return own + left + right + far + other
 
 
 def statistics(grad, weight, row_state, col_state):

time: 202 us -> 201 us (level)
    ppermute x37 -> x38, waiting for transfers between devices: 72.6 us -> 69.8 us  [send(): return lax.ppermute(value, 'dp', perm)]
    ppermute x37 -> x38, starting transfers between devices: 66.7 us -> 69 us  [send(): return lax.ppermute(value, 'dp', perm)]
    ppermute x12, starting transfers between devices: 22.9 us -> 20.8 us  [sum4(): second, third, fourth = (lax.ppermute(value, axis, perm) for perm in perms)]
  transfers between devices with their start and end apart: 49 -> 50, of which waited for: 22 -> 23; matrix products, arithmetic and copies ran while one was open for 4% -> 4% of each run, Pallas kernels for 3% -> 3%
where the time goes in v2:
time: 201 us; the launch traced here: 200 us
  starting transfers between devices  89.8 us (45%)
  waiting for transfers between devices  79.6 us (40%)
  other arithmetic  10.4 us (5%)
  Pallas kernels  10.3 us (5%)
  local copies, waits for them, and re-layouts  9.04 us (4%)
    ppermute x38, waiting for transfers between devices, send(): return lax.ppermute(value, 'dp', perm)  69.8 us
    ppermute x38, starting transfers between devices, send(): return lax.ppermute(value, 'dp', perm)  69 us
    ppermute x12, starting transfers between devices, sum4(): second, third, fourth = (lax.ppermute(value, axis, perm) for perm in perms)  20.8 us
    pallas_call x2, Pallas kernels, put(): pl.pallas_call(functools.partial(place_kernel, slabs), out_shape=jax.Shap...  10.3 us
    ppermute x12, waiting for transfers between devices, sum4(): second, third, fourth = (lax.ppermute(value, axis, perm) for perm in perms)  9.82 us
  transfers between devices with their start and end apart: 50, of which 23 were waited for; matrix products, arithmetic and copies ran while one was open for 4% of the time, Pallas kernels for 3%

profile of v2, /device:TPU:1, one launch (start us, length us, event | category | flops | bytes accessed | tf_op | source)
XLA Modules:
  0.0 200.4 jit_solution(15142243945595943350)
XLA Ops:
  1.9 3.3 %collective-permute-start = (f32[2,1,1,1,1,64,1280]{6,5,4,3,2,1,0:T(8,128)S(1)}, f32[2,1,1,1,1,64,1280]{6,5,4,3,2,1,0:T(8,128)S(1)}, u32[]{:S(2)}, u32[]{:S(2)}) collective-permute-start(f32[2,1,1,1,1,64,1280]{6,5,4,3,2,1,0:T(8,128)S(1)} %constant_dynamic-slice_fusion.3), channel_id=1, source_target_pairs={{0,16},{16,0},{32,48},{48,32},{64,80},{80,64},{96,112},{112,96},{1... | collective-permute-start | bytes 1966088 | tf_op jit(solution)/shard_map/ppermute | solution.py:36
  10.0 2.7 %collective-permute-start.3 = (f32[64,1280]{1,0:T(8,128)S(1)}, f32[64,1280]{1,0:T(8,128)S(1)}, u32[]{:S(2)}, u32[]{:S(2)}) collective-permute-start(f32[64,1280]{1,0:T(8,128)S(1)} %get-tuple-element.34), channel_id=1, source_target_pairs={{0,96},{16,112},{32,0},{48,16},{64,32},{80,48},{96,64},{112,80},{1... | collective-permute-start | bytes 983048 | tf_op jit(solution)/shard_map/ppermute | solution.py:36
  13.9 6.3 %collective-permute-done.2 = f32[64,1280]{1,0:T(8,128)S(1)} collective-permute-done((f32[64,1280]{1,0:T(8,128)S(1)}, f32[64,1280]{1,0:T(8,128)S(1)}, u32[]{:S(2)}, u32[]{:S(2)}) %collective-permute-start.2) | collective-permute-done | bytes 327712 | tf_op jit(solution)/shard_map/ppermute | solution.py:36
  23.9 2.7 %collective-permute-start.9 = (f32[128,1280]{1,0:T(8,128)S(1)}, f32[128,1280]{1,0:T(8,128)S(1)}, u32[]{:S(2)}, u32[]{:S(2)}) collective-permute-start(f32[128,1280]{1,0:T(8,128)S(1)} %get-tuple-element.37), channel_id=1, source_target_pairs={{0,96},{16,112},{32,0},{48,16},{64,32},{80,48},{96,64},{112,80},{1... | collective-permute-start | bytes 1966088 | tf_op jit(solution)/shard_map/ppermute | solution.py:36
  30.0 11.3 %collective-permute-done.10 = f32[128,1280]{1,0:T(8,128)S(1)} collective-permute-done((f32[128,1280]{1,0:T(8,128)S(1)}, f32[128,1280]{1,0:T(8,128)S(1)}, u32[]{:S(2)}, u32[]{:S(2)}) %collective-permute-start.10) | collective-permute-done | bytes 655392 | tf_op jit(solution)/shard_map/ppermute | solution.py:36
  48.5 5.2 %collective-permute-start.15 = (f32[2,64,1280]{2,1,0:T(8,128)S(1)}, f32[2,64,1280]{2,1,0:T(8,128)S(1)}, u32[]{:S(2)}, u32[]{:S(2)}) collective-permute-start(f32[2,64,1280]{2,1,0:T(8,128)S(1)} %pad_maximum_fusion.4), channel_id=1, source_target_pairs={{0,128},{16,144},{32,160},{48,176},{64,192},{80,208},{96,224},{112... | collective-permute-start | bytes 1966088 | tf_op jit(solution)/shard_map/ppermute | solution.py:36
  53.7 2.9 %collective-permute-start.14 = (f32[64,1280]{1,0:T(8,128)S(1)}, f32[64,1280]{1,0:T(8,128)S(1)}, u32[]{:S(2)}, u32[]{:S(2)}) collective-permute-start(f32[64,1280]{1,0:T(8,128)S(1)} %get-tuple-element.46), channel_id=1, source_target_pairs={{0,64},{16,80},{32,96},{48,112},{64,0},{80,16},{96,32},{112,48},{1... | collective-permute-start | bytes 983048 | tf_op jit(solution)/shard_map/ppermute | solution.py:36
  56.7 12.8 %collective-permute-done.13 = f32[64,1280]{1,0:T(8,128)S(1)} collective-permute-done((f32[64,1280]{1,0:T(8,128)S(1)}, f32[64,1280]{1,0:T(8,128)S(1)}, u32[]{:S(2)}, u32[]{:S(2)}) %collective-permute-start.13) | collective-permute-done | bytes 327712 | tf_op jit(solution)/shard_map/ppermute | solution.py:36
  69.4 7.0 %collective-permute-done.14 = f32[64,1280]{1,0:T(8,128)S(1)} collective-permute-done((f32[64,1280]{1,0:T(8,128)S(1)}, f32[64,1280]{1,0:T(8,128)S(1)}, u32[]{:S(2)}, u32[]{:S(2)}) %collective-permute-start.14) | collective-permute-done | bytes 327712 | tf_op jit(solution)/shard_map/ppermute | solution.py:36
  79.4 3.7 %collective-permute-start.17 = (f32[2,64]{1,0:T(2,128)S(1)}, f32[2,64]{1,0:T(2,128)S(1)}, u32[]{:S(2)}, u32[]{:S(2)}) collective-permute-start(f32[2,64]{1,0:T(2,128)S(1)} %get-tuple-element.70), channel_id=1, source_target_pairs={{0,1},{1,2},{2,3},{3,0},{4,5},{5,6},{6,7},{7,4},{8,9},{9,10},{10,1... | collective-permute-start | bytes 1544 | tf_op jit(solution)/shard_map/ppermute | solution.py:40
  91.0 3.0 %collective-permute-done.19 = f32[8,1280]{1,0:T(8,128)S(1)} collective-permute-done((f32[8,1280]{1,0:T(8,128)S(1)}, f32[8,1280]{1,0:T(8,128)S(1)}, u32[]{:S(2)}, u32[]{:S(2)}) %collective-permute-start.19) | collective-permute-done | bytes 40992 | tf_op jit(solution)/shard_map/ppermute | solution.py:40
  94.0 2.9 %collective-permute-start.24 = (f32[8,1280]{1,0:T(8,128)S(1)}, f32[8,1280]{1,0:T(8,128)S(1)}, u32[]{:S(2)}, u32[]{:S(2)}) collective-permute-start(f32[8,1280]{1,0:T(8,128)S(1)} %add_add_fusion.1), channel_id=1, source_target_pairs={{0,12},{4,0},{8,4},{12,8},{1,13},{5,1},{9,5},{13,9},{2,14},{6,2},{... | collective-permute-start | bytes 122888 | tf_op jit(solution)/shard_map/ppermute | solution.py:40
  98.5 2.9 %collective-permute-done.23 = f32[8,1280]{1,0:T(8,128)S(1)} collective-permute-done((f32[8,1280]{1,0:T(8,128)S(1)}, f32[8,1280]{1,0:T(8,128)S(1)}, u32[]{:S(2)}, u32[]{:S(2)}) %collective-permute-start.23) | collective-permute-done | bytes 40992 | tf_op jit(solution)/shard_map/ppermute | solution.py:40
  101.4 6.3 %collective-permute-start.25 = (f32[8,1280]{1,0:T(8,128)S(1)}, f32[8,1280]{1,0:T(8,128)S(1)}, u32[]{:S(2)}, u32[]{:S(2)}) collective-permute-start(f32[8,1280]{1,0:T(8,128)S(1)} %add_add_fusion), channel_id=1, source_target_pairs={{0,16},{16,0},{32,48},{48,32},{64,80},{80,64},{96,112},{112,96},{1... | collective-permute-start | bytes 122888 | tf_op jit(solution)/shard_map/ppermute | solution.py:36
  108.5 5.6 %collective-permute-start.26 = (f32[8,1280]{1,0:T(8,128)S(1)}, f32[8,1280]{1,0:T(8,128)S(1)}, u32[]{:S(2)}, u32[]{:S(2)}) collective-permute-start(f32[8,1280]{1,0:T(8,128)S(1)} %add.790), channel_id=1, source_target_pairs={{0,128},{16,144},{32,160},{48,176},{64,192},{80,208},{96,224},{112... | collective-permute-start | bytes 122888 | tf_op jit(solution)/shard_map/ppermute | solution.py:36
  122.8 3.2 %collective-permute-start.33 = (f32[2,64,1280]{2,1,0:T(8,128)S(1)}, f32[2,64,1280]{2,1,0:T(8,128)S(1)}, u32[]{:S(2)}, u32[]{:S(2)}) collective-permute-start(f32[2,64,1280]{2,1,0:T(8,128)S(1)} %multiply_subtract_fusion), channel_id=1, source_target_pairs={{0,16},{16,0},{32,48},{48,32},{64,80},{80,64},{96,112},{112,96},{1... | collective-permute-start | bytes 1966088 | tf_op jit(solution)/shard_map/ppermute | solution.py:36
  127.6 6.2 %collective-permute-start.32 = (f32[64,1280]{1,0:T(8,128)S(1)}, f32[64,1280]{1,0:T(8,128)S(1)}, u32[]{:S(2)}, u32[]{:S(2)}) collective-permute-start(f32[64,1280]{1,0:T(8,128)S(1)} %get-tuple-element.91), channel_id=1, source_target_pairs={{0,128},{16,144},{32,160},{48,176},{64,192},{80,208},{96,224},{112... | collective-permute-start | bytes 983048 | tf_op jit(solution)/shard_map/ppermute | solution.py:36
  133.7 12.5 %collective-permute-done.32 = f32[64,1280]{1,0:T(8,128)S(1)} collective-permute-done((f32[64,1280]{1,0:T(8,128)S(1)}, f32[64,1280]{1,0:T(8,128)S(1)}, u32[]{:S(2)}, u32[]{:S(2)}) %collective-permute-start.32) | collective-permute-done | bytes 327712 | tf_op jit(solution)/shard_map/ppermute | solution.py:36
  149.2 5.1 %collective-permute-start.39 = (f32[64,1280]{1,0:T(8,128)S(1)}, f32[64,1280]{1,0:T(8,128)}, u32[]{:S(2)}, u32[]{:S(2)}) collective-permute-start(f32[64,1280]{1,0:T(8,128)S(1)} %get-tuple-element.90), channel_id=1, source_target_pairs={{0,128},{16,144},{32,160},{48,176},{64,192},{80,208},{96,224},{112... | collective-permute-start | bytes 983048 | tf_op jit(solution)/shard_map/ppermute | solution.py:36
  156.7 5.9 %collective-permute-done.39 = f32[64,1280]{1,0:T(8,128)} collective-permute-done((f32[64,1280]{1,0:T(8,128)S(1)}, f32[64,1280]{1,0:T(8,128)}, u32[]{:S(2)}, u32[]{:S(2)}) %collective-permute-start.39) | collective-permute-done | bytes 327712 | tf_op jit(solution)/shard_map/ppermute | solution.py:36
  162.5 5.0 %collective-permute-start.35 = (f32[2,64,1280]{2,1,0:T(8,128)S(1)}, f32[2,64,1280]{2,1,0:T(8,128)S(1)}, u32[]{:S(2)}, u32[]{:S(2)}) collective-permute-start(f32[2,64,1280]{2,1,0:T(8,128)S(1)} %collective-permute-done.31), channel_id=1, source_target_pairs={{0,16},{16,0},{32,48},{48,32},{64,80},{80,64},{96,112},{112,96},{1... | collective-permute-start | bytes 1966088 | tf_op jit(solution)/shard_map/ppermute | solution.py:36
  179.5 7.0 %shard_map.67.refs_8_ = f32[2048,1280]{1,0:T(8,128)} custom-call(s32[24]{0:T(128)} %stack.162.where, f32[128,1280]{1,0:T(8,128)} %bitcast.126, f32[128,1280]{1,0:T(8,128)} %bitcast.129, f32[128,1280]{1,0:T(8,128)} %bitcast.128, f32[128,1280]{1,0:T(8,128)} %bitcast.130, f32[128,1280]{1,0:T(8,128)} %bitcast.127, f32[128,1280]{1,0:T(8,128)} %bitcast.131, ...), custom_call_target="tpu_custom_call" | custom-call | tf_op jit(solution)/shard_map/pallas_call | solution.py:177
  186.5 5.6 %collective-permute-done.44.refs_2_ = f32[64,1280]{1,0:T(8,128)} collective-permute-done((f32[64,1280]{1,0:T(8,128)}, f32[64,1280]{1,0:T(8,128)}, u32[]{:S(2)}, u32[]{:S(2)}) %collective-permute-start.44) | collective-permute-done | bytes 327712 | tf_op jit(solution)/shard_map/ppermute | solution.py:36
  197.0 3.3 %shard_map.68 = f32[2048,1280]{1,0:T(8,128)} custom-call(s32[8]{0:T(128)} %stack.137.where, f32[64,1280]{1,0:T(8,128)} %collective-permute-done.43.refs_0_, f32[64,1280]{1,0:T(8,128)} %copy-done.11, f32[64,1280]{1,0:T(8,128)} %collective-permute-done.44.refs_2_, f32[64,1280]{1,0:T(8,128)} %copy-done.12, ...), custom_call_target="tpu_custom_call", output_to_operand_aliasing={{}: (9, {})} | custom-call | tf_op jit(solution)/shard_map/pallas_call | solution.py:177
  (153 shorter events, 67.2 us)
Async XLA Ops:
  10.0 10.3 %collective-permute-start.2 = (f32[64,1280]{1,0:T(8,128)S(1)}, f32[64,1280]{1,0:T(8,128)S(1)}, u32[]{:S(2)}, u32[]{:S(2)}) collective-permute-start(f32[64,1280]{1,0:T(8,128)S(1)} %get-tuple-element.33), channel_id=1, source_target_pairs={{0,32},{16,48},{32,64},{48,80},{64,96},{80,112},{96,0},{112,16},{1... | collective-permute-start | bytes 983048 | tf_op jit(solution)/shard_map/ppermute | solution.py:36
  23.9 17.4 %collective-permute-start.10 = (f32[128,1280]{1,0:T(8,128)S(1)}, f32[128,1280]{1,0:T(8,128)S(1)}, u32[]{:S(2)}, u32[]{:S(2)}) collective-permute-start(f32[128,1280]{1,0:T(8,128)S(1)} %get-tuple-element.36), channel_id=1, source_target_pairs={{0,32},{16,48},{32,64},{48,80},{64,96},{80,112},{96,0},{112,16},{1... | collective-permute-start | bytes 1966088 | tf_op jit(solution)/shard_map/ppermute | solution.py:36
  23.9 18.4 %collective-permute-start.9 = (f32[128,1280]{1,0:T(8,128)S(1)}, f32[128,1280]{1,0:T(8,128)S(1)}, u32[]{:S(2)}, u32[]{:S(2)}) collective-permute-start(f32[128,1280]{1,0:T(8,128)S(1)} %get-tuple-element.37), channel_id=1, source_target_pairs={{0,96},{16,112},{32,0},{48,16},{64,32},{80,48},{96,64},{112,80},{1... | collective-permute-start | bytes 1966088 | tf_op jit(solution)/shard_map/ppermute | solution.py:36
  28.7 13.5 %collective-permute-start.8 = (f32[2,1,1,1,1,64,1280]{6,5,4,3,2,1,0:T(8,128)S(1)}, f32[2,1,1,1,1,64,1280]{6,5,4,3,2,1,0:T(8,128)S(1)}, u32[]{:S(2)}, u32[]{:S(2)}) collective-permute-start(f32[2,1,1,1,1,64,1280]{6,5,4,3,2,1,0:T(8,128)S(1)} %get-tuple-element.76), channel_id=1, source_target_pairs={{0,16},{16,0},{32,48},{48,32},{64,80},{80,64},{96,112},{112,96},{1... | collective-permute-start | bytes 1966088 | tf_op jit(solution)/shard_map/ppermute | solution.py:36
  29.5 14.0 %collective-permute-start.5 = (f32[2,1,1,1,1,64,1280]{6,5,0,4,3,2,1:T(8,128)S(1)}, f32[2,1,1,1,1,64,1280]{6,5,0,4,3,2,1:T(8,128)S(1)}, u32[]{:S(2)}, u32[]{:S(2)}) collective-permute-start(f32[2,1,1,1,1,64,1280]{6,5,0,4,3,2,1:T(8,128)S(1)} %get-tuple-element.77), channel_id=1, source_target_pairs={{0,16},{16,0},{32,48},{48,32},{64,80},{80,64},{96,112},{112,96},{1... | collective-permute-start | bytes 1966088 | tf_op jit(solution)/shard_map/ppermute | solution.py:36
  29.6 14.0 %collective-permute-start.4 = (f32[2,1,1,1,1,64,1280]{6,5,0,4,3,2,1:T(8,128)S(1)}, f32[2,1,1,1,1,64,1280]{6,5,0,4,3,2,1:T(8,128)S(1)}, u32[]{:S(2)}, u32[]{:S(2)}) collective-permute-start(f32[2,1,1,1,1,64,1280]{6,5,0,4,3,2,1:T(8,128)S(1)} %get-tuple-element.78), channel_id=1, source_target_pairs={{0,16},{16,0},{32,48},{48,32},{64,80},{80,64},{96,112},{112,96},{1... | collective-permute-start | bytes 1966088 | tf_op jit(solution)/shard_map/ppermute | solution.py:36
  45.8 30.7 %collective-permute-start.11 = (f32[2,64,1280]{2,1,0:T(8,128)S(1)}, f32[2,64,1280]{2,1,0:T(8,128)S(1)}, u32[]{:S(2)}, u32[]{:S(2)}) collective-permute-start(f32[2,64,1280]{2,1,0:T(8,128)S(1)} %get-tuple-element.43), channel_id=1, source_target_pairs={{0,32},{16,48},{32,64},{48,80},{64,96},{80,112},{96,0},{112,16},{1... | collective-permute-start | bytes 1966088 | tf_op jit(solution)/shard_map/ppermute | solution.py:36
  45.9 30.6 %collective-permute-start.12 = (f32[2,64,1280]{2,1,0:T(8,128)S(1)}, f32[2,64,1280]{2,1,0:T(8,128)S(1)}, u32[]{:S(2)}, u32[]{:S(2)}) collective-permute-start(f32[2,64,1280]{2,1,0:T(8,128)S(1)} %get-tuple-element.44), channel_id=1, source_target_pairs={{0,96},{16,112},{32,0},{48,16},{64,32},{80,48},{96,64},{112,80},{1... | collective-permute-start | bytes 1966088 | tf_op jit(solution)/shard_map/ppermute | solution.py:36
  48.5 27.9 %collective-permute-start.15 = (f32[2,64,1280]{2,1,0:T(8,128)S(1)}, f32[2,64,1280]{2,1,0:T(8,128)S(1)}, u32[]{:S(2)}, u32[]{:S(2)}) collective-permute-start(f32[2,64,1280]{2,1,0:T(8,128)S(1)} %pad_maximum_fusion.4), channel_id=1, source_target_pairs={{0,128},{16,144},{32,160},{48,176},{64,192},{80,208},{96,224},{112... | collective-permute-start | bytes 1966088 | tf_op jit(solution)/shard_map/ppermute | solution.py:36
  53.7 15.7 %collective-permute-start.13 = (f32[64,1280]{1,0:T(8,128)S(1)}, f32[64,1280]{1,0:T(8,128)S(1)}, u32[]{:S(2)}, u32[]{:S(2)}) collective-permute-start(f32[64,1280]{1,0:T(8,128)S(1)} %get-tuple-element.45), channel_id=1, source_target_pairs={{0,64},{16,80},{32,96},{48,112},{64,0},{80,16},{96,32},{112,48},{1... | collective-permute-start | bytes 983048 | tf_op jit(solution)/shard_map/ppermute | solution.py:36
  53.7 22.7 %collective-permute-start.14 = (f32[64,1280]{1,0:T(8,128)S(1)}, f32[64,1280]{1,0:T(8,128)S(1)}, u32[]{:S(2)}, u32[]{:S(2)}) collective-permute-start(f32[64,1280]{1,0:T(8,128)S(1)} %get-tuple-element.46), channel_id=1, source_target_pairs={{0,64},{16,80},{32,96},{48,112},{64,0},{80,16},{96,32},{112,48},{1... | collective-permute-start | bytes 983048 | tf_op jit(solution)/shard_map/ppermute | solution.py:36
  122.8 23.4 %collective-permute-start.33 = (f32[2,64,1280]{2,1,0:T(8,128)S(1)}, f32[2,64,1280]{2,1,0:T(8,128)S(1)}, u32[]{:S(2)}, u32[]{:S(2)}) collective-permute-start(f32[2,64,1280]{2,1,0:T(8,128)S(1)} %multiply_subtract_fusion), channel_id=1, source_target_pairs={{0,16},{16,0},{32,48},{48,32},{64,80},{80,64},{96,112},{112,96},{1... | collective-permute-start | bytes 1966088 | tf_op jit(solution)/shard_map/ppermute | solution.py:36
  126.1 20.2 %collective-permute-start.31 = (f32[2,64,1280]{2,1,0:T(8,128)S(1)}, f32[2,64,1280]{2,1,0:T(8,128)S(1)}, u32[]{:S(2)}, u32[]{:S(2)}) collective-permute-start(f32[2,64,1280]{2,1,0:T(8,128)S(1)} %multiply_subtract_fusion), channel_id=1, source_target_pairs={{0,96},{16,112},{32,0},{48,16},{64,32},{80,48},{96,64},{112,80},{1... | collective-permute-start | bytes 1966088 | tf_op jit(solution)/shard_map/ppermute | solution.py:36
  126.1 20.2 %collective-permute-start.30 = (f32[2,64,1280]{2,1,0:T(8,128)S(1)}, f32[2,64,1280]{2,1,0:T(8,128)S(1)}, u32[]{:S(2)}, u32[]{:S(2)}) collective-permute-start(f32[2,64,1280]{2,1,0:T(8,128)S(1)} %multiply_subtract_fusion), channel_id=1, source_target_pairs={{0,32},{16,48},{32,64},{48,80},{64,96},{80,112},{96,0},{112,16},{1... | collective-permute-start | bytes 1966088 | tf_op jit(solution)/shard_map/ppermute | solution.py:36
  127.6 18.7 %collective-permute-start.32 = (f32[64,1280]{1,0:T(8,128)S(1)}, f32[64,1280]{1,0:T(8,128)S(1)}, u32[]{:S(2)}, u32[]{:S(2)}) collective-permute-start(f32[64,1280]{1,0:T(8,128)S(1)} %get-tuple-element.91), channel_id=1, source_target_pairs={{0,128},{16,144},{32,160},{48,176},{64,192},{80,208},{96,224},{112... | collective-permute-start | bytes 983048 | tf_op jit(solution)/shard_map/ppermute | solution.py:36
  146.5 22.9 %collective-permute-start.36 = (f32[128,1280]{1,0:T(8,128)S(1)}, f32[128,1280]{1,0:T(8,128)S(1)}, u32[]{:S(2)}, u32[]{:S(2)}) collective-permute-start(f32[128,1280]{1,0:T(8,128)S(1)} %get-tuple-element.52), channel_id=1, source_target_pairs={{0,32},{16,48},{32,64},{48,80},{64,96},{80,112},{96,0},{112,16},{1... | collective-permute-start | bytes 1966088 | tf_op jit(solution)/shard_map/ppermute | solution.py:36
  146.9 23.2 %collective-permute-start.37 = (f32[128,1280]{1,0:T(8,128)S(1)}, f32[128,1280]{1,0:T(8,128)}, u32[]{:S(2)}, u32[]{:S(2)}) collective-permute-start(f32[128,1280]{1,0:T(8,128)S(1)} %get-tuple-element.53), channel_id=1, source_target_pairs={{0,96},{16,112},{32,0},{48,16},{64,32},{80,48},{96,64},{112,80},{1... | collective-permute-start | bytes 1966088 | tf_op jit(solution)/shard_map/ppermute | solution.py:36
  149.2 13.3 %collective-permute-start.39 = (f32[64,1280]{1,0:T(8,128)S(1)}, f32[64,1280]{1,0:T(8,128)}, u32[]{:S(2)}, u32[]{:S(2)}) collective-permute-start(f32[64,1280]{1,0:T(8,128)S(1)} %get-tuple-element.90), channel_id=1, source_target_pairs={{0,128},{16,144},{32,160},{48,176},{64,192},{80,208},{96,224},{112... | collective-permute-start | bytes 983048 | tf_op jit(solution)/shard_map/ppermute | solution.py:36
  154.3 15.1 %collective-permute-start.38 = (f32[64,1280]{1,0:T(8,128)S(1)}, f32[64,1280]{1,0:T(8,128)S(1)}, u32[]{:S(2)}, u32[]{:S(2)}) collective-permute-start(f32[64,1280]{1,0:T(8,128)S(1)} %collective-permute-done.32), channel_id=1, source_target_pairs={{0,64},{16,80},{32,96},{48,112},{64,0},{80,16},{96,32},{112,48},{1... | collective-permute-start | bytes 983048 | tf_op jit(solution)/shard_map/ppermute | solution.py:36
  154.3 19.9 %collective-permute-start.34 = (f32[2,64,1280]{2,1,0:T(8,128)S(1)}, f32[2,64,1280]{2,1,0:T(8,128)S(1)}, u32[]{:S(2)}, u32[]{:S(2)}) collective-permute-start(f32[2,64,1280]{2,1,0:T(8,128)S(1)} %collective-permute-done.30), channel_id=1, source_target_pairs={{0,16},{16,0},{32,48},{48,32},{64,80},{80,64},{96,112},{112,96},{1... | collective-permute-start | bytes 1966088 | tf_op jit(solution)/shard_map/ppermute | solution.py:36
  162.5 12.5 %collective-permute-start.35 = (f32[2,64,1280]{2,1,0:T(8,128)S(1)}, f32[2,64,1280]{2,1,0:T(8,128)S(1)}, u32[]{:S(2)}, u32[]{:S(2)}) collective-permute-start(f32[2,64,1280]{2,1,0:T(8,128)S(1)} %collective-permute-done.31), channel_id=1, source_target_pairs={{0,16},{16,0},{32,48},{48,32},{64,80},{80,64},{96,112},{112,96},{1... | collective-permute-start | bytes 1966088 | tf_op jit(solution)/shard_map/ppermute | solution.py:36
  174.2 12.3 %collective-permute-start.45 = (f32[64,1280]{1,0:T(8,128)}, f32[64,1280]{1,0:T(8,128)}, u32[]{:S(2)}, u32[]{:S(2)}) collective-permute-start(f32[64,1280]{1,0:T(8,128)} %collective-permute-done.39), channel_id=1, source_target_pairs={{0,64},{16,80},{32,96},{48,112},{64,0},{80,16},{96,32},{112,48},{1... | collective-permute-start | bytes 983048 | tf_op jit(solution)/shard_map/ppermute | solution.py:36
  175.0 17.1 %collective-permute-start.44 = (f32[64,1280]{1,0:T(8,128)}, f32[64,1280]{1,0:T(8,128)}, u32[]{:S(2)}, u32[]{:S(2)}) collective-permute-start(f32[64,1280]{1,0:T(8,128)} %collective-permute-done.39), channel_id=1, source_target_pairs={{0,96},{16,112},{32,0},{48,16},{64,32},{80,48},{96,64},{112,80},{1... | collective-permute-start | bytes 983048 | tf_op jit(solution)/shard_map/ppermute | solution.py:36
  178.4 14.3 %collective-permute-start.43 = (f32[64,1280]{1,0:T(8,128)}, f32[64,1280]{1,0:T(8,128)}, u32[]{:S(2)}, u32[]{:S(2)}) collective-permute-start(f32[64,1280]{1,0:T(8,128)} %collective-permute-done.39), channel_id=1, source_target_pairs={{0,32},{16,48},{32,64},{48,80},{64,96},{80,112},{96,0},{112,16},{1... | collective-permute-start | bytes 983048 | tf_op jit(solution)/shard_map/ppermute | solution.py:36
  (45 other events, 683.2 us)

commit v3 on v2

--- a/solution.py
+++ b/solution.py
@@ -210,10 +210,12 @@
 
     both = lambda dz, dx: [(e, dz, dx) for e in range(E)]
     other = [send(shard[e], ZHALF) for e in range(E)]
-    left, right = send(shard, PLUS), send(shard, MINUS)
+    left = send(shard, PLUS)
+    right = [send(shard[e], MINUS) for e in range(E)]
     shard_c = send(shard, CORE)
 
     left, right, other_0, shard_c = lax.optimization_barrier((left, right, other[0], shard_c))
+    right = jnp.stack(right)
     plus = jnp.concatenate([left[0], other_0])
     minus = jnp.concatenate([right[1], other_0])
     plus, minus = lax.optimization_barrier((plus, minus))

time: 201 us -> 202 us (level)
  starting transfers between devices: 89.8 us -> 92.9 us
    ppermute x38 -> x39, starting transfers between devices: 69 us -> 72.1 us  [send(): return lax.ppermute(value, 'dp', perm)]
    ppermute x38 -> x39, waiting for transfers between devices: 69.8 us -> 68.7 us  [send(): return lax.ppermute(value, 'dp', perm)]
  transfers between devices with their start and end apart: 50 -> 51, of which waited for: 23 -> 23; matrix products, arithmetic and copies ran while one was open for 4% -> 4% of each run, Pallas kernels for 3% -> 3%
where the time goes in v3:
time: 202 us
  starting transfers between devices  92.9 us (46%)
  waiting for transfers between devices  78.6 us (39%)
  other arithmetic  10.4 us (5%)
  Pallas kernels  10.3 us (5%)
  local copies, waits for them, and re-layouts  8.27 us (4%)
    ppermute x39, starting transfers between devices, send(): return lax.ppermute(value, 'dp', perm)  72.1 us
    ppermute x39, waiting for transfers between devices, send(): return lax.ppermute(value, 'dp', perm)  68.7 us
    ppermute x12, starting transfers between devices, sum4(): second, third, fourth = (lax.ppermute(value, axis, perm) for perm in perms)  20.8 us
    pallas_call x2, Pallas kernels, put(): pl.pallas_call(functools.partial(place_kernel, slabs), out_shape=jax.Shap...  10.3 us
    ppermute x12, waiting for transfers between devices, sum4(): second, third, fourth = (lax.ppermute(value, axis, perm) for perm in perms)  9.82 us
  transfers between devices with their start and end apart: 51, of which 23 were waited for; matrix products, arithmetic and copies ran while one was open for 4% of the time, Pallas kernels for 3%

profile of v3, /device:TPU:1, one launch (start us, length us, event | category | flops | bytes accessed | tf_op | source)
XLA Modules:
  0.0 201.7 jit_solution(18194938886661342800)
XLA Ops:
  1.9 3.3 %collective-permute-start = (f32[2,1,1,1,1,64,1280]{6,5,4,3,2,1,0:T(8,128)S(1)}, f32[2,1,1,1,1,64,1280]{6,5,4,3,2,1,0:T(8,128)S(1)}, u32[]{:S(2)}, u32[]{:S(2)}) collective-permute-start(f32[2,1,1,1,1,64,1280]{6,5,4,3,2,1,0:T(8,128)S(1)} %constant_dynamic-slice_fusion.3), channel_id=1, source_target_pairs={{0,16},{16,0},{32,48},{48,32},{64,80},{80,64},{96,112},{112,96},{1... | collective-permute-start | bytes 1966088 | tf_op jit(solution)/shard_map/ppermute | solution.py:36
  13.9 6.3 %collective-permute-done.2 = f32[64,1280]{1,0:T(8,128)S(1)} collective-permute-done((f32[64,1280]{1,0:T(8,128)S(1)}, f32[64,1280]{1,0:T(8,128)S(1)}, u32[]{:S(2)}, u32[]{:S(2)}) %collective-permute-start.2) | collective-permute-done | bytes 327712 | tf_op jit(solution)/shard_map/ppermute | solution.py:36
  30.0 11.3 %collective-permute-done.10 = f32[128,1280]{1,0:T(8,128)S(1)} collective-permute-done((f32[128,1280]{1,0:T(8,128)S(1)}, f32[128,1280]{1,0:T(8,128)S(1)}, u32[]{:S(2)}, u32[]{:S(2)}) %collective-permute-start.10) | collective-permute-done | bytes 655392 | tf_op jit(solution)/shard_map/ppermute | solution.py:36
  48.5 5.2 %collective-permute-start.15 = (f32[2,64,1280]{2,1,0:T(8,128)S(1)}, f32[2,64,1280]{2,1,0:T(8,128)S(1)}, u32[]{:S(2)}, u32[]{:S(2)}) collective-permute-start(f32[2,64,1280]{2,1,0:T(8,128)S(1)} %pad_maximum_fusion.4), channel_id=1, source_target_pairs={{0,128},{16,144},{32,160},{48,176},{64,192},{80,208},{96,224},{112... | collective-permute-start | bytes 1966088 | tf_op jit(solution)/shard_map/ppermute | solution.py:36
  53.7 2.9 %collective-permute-start.14 = (f32[64,1280]{1,0:T(8,128)S(1)}, f32[64,1280]{1,0:T(8,128)S(1)}, u32[]{:S(2)}, u32[]{:S(2)}) collective-permute-start(f32[64,1280]{1,0:T(8,128)S(1)} %get-tuple-element.47), channel_id=1, source_target_pairs={{0,64},{16,80},{32,96},{48,112},{64,0},{80,16},{96,32},{112,48},{1... | collective-permute-start | bytes 983048 | tf_op jit(solution)/shard_map/ppermute | solution.py:36
  56.7 12.8 %collective-permute-done.13 = f32[64,1280]{1,0:T(8,128)S(1)} collective-permute-done((f32[64,1280]{1,0:T(8,128)S(1)}, f32[64,1280]{1,0:T(8,128)S(1)}, u32[]{:S(2)}, u32[]{:S(2)}) %collective-permute-start.13) | collective-permute-done | bytes 327712 | tf_op jit(solution)/shard_map/ppermute | solution.py:36
  69.4 7.0 %collective-permute-done.14 = f32[64,1280]{1,0:T(8,128)S(1)} collective-permute-done((f32[64,1280]{1,0:T(8,128)S(1)}, f32[64,1280]{1,0:T(8,128)S(1)}, u32[]{:S(2)}, u32[]{:S(2)}) %collective-permute-start.14) | collective-permute-done | bytes 327712 | tf_op jit(solution)/shard_map/ppermute | solution.py:36
  79.4 3.7 %collective-permute-start.17 = (f32[2,64]{1,0:T(2,128)S(1)}, f32[2,64]{1,0:T(2,128)S(1)}, u32[]{:S(2)}, u32[]{:S(2)}) collective-permute-start(f32[2,64]{1,0:T(2,128)S(1)} %get-tuple-element.72), channel_id=1, source_target_pairs={{0,1},{1,2},{2,3},{3,0},{4,5},{5,6},{6,7},{7,4},{8,9},{9,10},{10,1... | collective-permute-start | bytes 1544 | tf_op jit(solution)/shard_map/ppermute | solution.py:40
  91.0 3.0 %collective-permute-done.19 = f32[8,1280]{1,0:T(8,128)S(1)} collective-permute-done((f32[8,1280]{1,0:T(8,128)S(1)}, f32[8,1280]{1,0:T(8,128)S(1)}, u32[]{:S(2)}, u32[]{:S(2)}) %collective-permute-start.19) | collective-permute-done | bytes 40992 | tf_op jit(solution)/shard_map/ppermute | solution.py:40
  94.0 2.9 %collective-permute-start.24 = (f32[8,1280]{1,0:T(8,128)S(1)}, f32[8,1280]{1,0:T(8,128)S(1)}, u32[]{:S(2)}, u32[]{:S(2)}) collective-permute-start(f32[8,1280]{1,0:T(8,128)S(1)} %add_add_fusion.1), channel_id=1, source_target_pairs={{0,12},{4,0},{8,4},{12,8},{1,13},{5,1},{9,5},{13,9},{2,14},{6,2},{... | collective-permute-start | bytes 122888 | tf_op jit(solution)/shard_map/ppermute | solution.py:40
  98.5 2.9 %collective-permute-done.23 = f32[8,1280]{1,0:T(8,128)S(1)} collective-permute-done((f32[8,1280]{1,0:T(8,128)S(1)}, f32[8,1280]{1,0:T(8,128)S(1)}, u32[]{:S(2)}, u32[]{:S(2)}) %collective-permute-start.23) | collective-permute-done | bytes 40992 | tf_op jit(solution)/shard_map/ppermute | solution.py:40
  101.4 6.3 %collective-permute-start.25 = (f32[8,1280]{1,0:T(8,128)S(1)}, f32[8,1280]{1,0:T(8,128)S(1)}, u32[]{:S(2)}, u32[]{:S(2)}) collective-permute-start(f32[8,1280]{1,0:T(8,128)S(1)} %add_add_fusion), channel_id=1, source_target_pairs={{0,16},{16,0},{32,48},{48,32},{64,80},{80,64},{96,112},{112,96},{1... | collective-permute-start | bytes 122888 | tf_op jit(solution)/shard_map/ppermute | solution.py:36
  108.5 5.6 %collective-permute-start.26 = (f32[8,1280]{1,0:T(8,128)S(1)}, f32[8,1280]{1,0:T(8,128)S(1)}, u32[]{:S(2)}, u32[]{:S(2)}) collective-permute-start(f32[8,1280]{1,0:T(8,128)S(1)} %add.790), channel_id=1, source_target_pairs={{0,128},{16,144},{32,160},{48,176},{64,192},{80,208},{96,224},{112... | collective-permute-start | bytes 122888 | tf_op jit(solution)/shard_map/ppermute | solution.py:36
  122.8 3.2 %collective-permute-start.34 = (f32[2,64,1280]{2,1,0:T(8,128)S(1)}, f32[2,64,1280]{2,1,0:T(8,128)S(1)}, u32[]{:S(2)}, u32[]{:S(2)}) collective-permute-start(f32[2,64,1280]{2,1,0:T(8,128)S(1)} %multiply_subtract_fusion), channel_id=1, source_target_pairs={{0,16},{16,0},{32,48},{48,32},{64,80},{80,64},{96,112},{112,96},{1... | collective-permute-start | bytes 1966088 | tf_op jit(solution)/shard_map/ppermute | solution.py:36
  126.1 3.0 %collective-permute-start.32 = (f32[64,1280]{1,0:T(8,128)S(1)}, f32[64,1280]{1,0:T(8,128)S(1)}, u32[]{:S(2)}, u32[]{:S(2)}) collective-permute-start(f32[64,1280]{1,0:T(8,128)S(1)} %get-tuple-element.92), channel_id=1, source_target_pairs={{0,96},{16,112},{32,0},{48,16},{64,32},{80,48},{96,64},{112,80},{1... | collective-permute-start | bytes 983048 | tf_op jit(solution)/shard_map/ppermute | solution.py:36
  129.1 6.1 %collective-permute-start.33 = (f32[64,1280]{1,0:T(8,128)S(1)}, f32[64,1280]{1,0:T(8,128)S(1)}, u32[]{:S(2)}, u32[]{:S(2)}) collective-permute-start(f32[64,1280]{1,0:T(8,128)S(1)} %get-tuple-element.93), channel_id=1, source_target_pairs={{0,128},{16,144},{32,160},{48,176},{64,192},{80,208},{96,224},{112... | collective-permute-start | bytes 983048 | tf_op jit(solution)/shard_map/ppermute | solution.py:36
  135.8 11.8 %collective-permute-done.33 = f32[64,1280]{1,0:T(8,128)S(1)} collective-permute-done((f32[64,1280]{1,0:T(8,128)S(1)}, f32[64,1280]{1,0:T(8,128)S(1)}, u32[]{:S(2)}, u32[]{:S(2)}) %collective-permute-start.33) | collective-permute-done | bytes 327712 | tf_op jit(solution)/shard_map/ppermute | solution.py:36
  150.6 5.1 %collective-permute-start.40 = (f32[64,1280]{1,0:T(8,128)S(1)}, f32[64,1280]{1,0:T(8,128)}, u32[]{:S(2)}, u32[]{:S(2)}) collective-permute-start(f32[64,1280]{1,0:T(8,128)S(1)} %get-tuple-element.92), channel_id=1, source_target_pairs={{0,128},{16,144},{32,160},{48,176},{64,192},{80,208},{96,224},{112... | collective-permute-start | bytes 983048 | tf_op jit(solution)/shard_map/ppermute | solution.py:36
  158.1 5.8 %collective-permute-done.40 = f32[64,1280]{1,0:T(8,128)} collective-permute-done((f32[64,1280]{1,0:T(8,128)S(1)}, f32[64,1280]{1,0:T(8,128)}, u32[]{:S(2)}, u32[]{:S(2)}) %collective-permute-start.40) | collective-permute-done | bytes 327712 | tf_op jit(solution)/shard_map/ppermute | solution.py:36
  163.9 5.0 %collective-permute-start.36 = (f32[2,64,1280]{2,1,0:T(8,128)S(1)}, f32[2,64,1280]{2,1,0:T(8,128)S(1)}, u32[]{:S(2)}, u32[]{:S(2)}) collective-permute-start(f32[2,64,1280]{2,1,0:T(8,128)S(1)} %pad_maximum_fusion.5), channel_id=1, source_target_pairs={{0,16},{16,0},{32,48},{48,32},{64,80},{80,64},{96,112},{112,96},{1... | collective-permute-start | bytes 1966088 | tf_op jit(solution)/shard_map/ppermute | solution.py:36
  170.4 2.9 %collective-permute-start.41 = (f32[128,1280]{1,0:T(8,128)S(1)}, f32[128,1280]{1,0:T(8,128)S(1)}, u32[]{:S(2)}, u32[]{:S(2)}) collective-permute-start(f32[128,1280]{1,0:T(8,128)S(1)} %collective-permute-done.37.refs_6_), channel_id=1, source_target_pairs={{0,16},{16,0},{32,48},{48,32},{64,80},{80,64},{96,112},{112,96},{1... | collective-permute-start | bytes 1966088 | tf_op jit(solution)/shard_map/ppermute | solution.py:36
  180.8 7.0 %shard_map.67.refs_8_ = f32[2048,1280]{1,0:T(8,128)} custom-call(s32[24]{0:T(128)} %stack.171.where, f32[128,1280]{1,0:T(8,128)} %bitcast.126, f32[128,1280]{1,0:T(8,128)} %bitcast.130, f32[128,1280]{1,0:T(8,128)} %bitcast.128, f32[128,1280]{1,0:T(8,128)} %bitcast.131, f32[128,1280]{1,0:T(8,128)} %bitcast.127, f32[128,1280]{1,0:T(8,128)} %bitcast.132, ...), custom_call_target="tpu_custom_call" | custom-call | tf_op jit(solution)/shard_map/pallas_call | solution.py:177
  187.9 5.6 %collective-permute-done.45.refs_2_ = f32[64,1280]{1,0:T(8,128)} collective-permute-done((f32[64,1280]{1,0:T(8,128)}, f32[64,1280]{1,0:T(8,128)}, u32[]{:S(2)}, u32[]{:S(2)}) %collective-permute-start.45) | collective-permute-done | bytes 327712 | tf_op jit(solution)/shard_map/ppermute | solution.py:36
  198.3 3.3 %shard_map.68 = f32[2048,1280]{1,0:T(8,128)} custom-call(s32[8]{0:T(128)} %stack.146.where, f32[64,1280]{1,0:T(8,128)} %collective-permute-done.44.refs_0_, f32[64,1280]{1,0:T(8,128)} %copy-done.11, f32[64,1280]{1,0:T(8,128)} %collective-permute-done.45.refs_2_, f32[64,1280]{1,0:T(8,128)} %copy-done.12, ...), custom_call_target="tpu_custom_call", output_to_operand_aliasing={{}: (9, {})} | custom-call | tf_op jit(solution)/shard_map/pallas_call | solution.py:177
  (155 shorter events, 68.7 us)
Async XLA Ops:
  10.0 10.3 %collective-permute-start.2 = (f32[64,1280]{1,0:T(8,128)S(1)}, f32[64,1280]{1,0:T(8,128)S(1)}, u32[]{:S(2)}, u32[]{:S(2)}) collective-permute-start(f32[64,1280]{1,0:T(8,128)S(1)} %get-tuple-element.34), channel_id=1, source_target_pairs={{0,32},{16,48},{32,64},{48,80},{64,96},{80,112},{96,0},{112,16},{1... | collective-permute-start | bytes 983048 | tf_op jit(solution)/shard_map/ppermute | solution.py:36
  23.9 17.4 %collective-permute-start.10 = (f32[128,1280]{1,0:T(8,128)S(1)}, f32[128,1280]{1,0:T(8,128)S(1)}, u32[]{:S(2)}, u32[]{:S(2)}) collective-permute-start(f32[128,1280]{1,0:T(8,128)S(1)} %get-tuple-element.37), channel_id=1, source_target_pairs={{0,32},{16,48},{32,64},{48,80},{64,96},{80,112},{96,0},{112,16},{1... | collective-permute-start | bytes 1966088 | tf_op jit(solution)/shard_map/ppermute | solution.py:36
  23.9 18.4 %collective-permute-start.9 = (f32[128,1280]{1,0:T(8,128)S(1)}, f32[128,1280]{1,0:T(8,128)S(1)}, u32[]{:S(2)}, u32[]{:S(2)}) collective-permute-start(f32[128,1280]{1,0:T(8,128)S(1)} %get-tuple-element.38), channel_id=1, source_target_pairs={{0,96},{16,112},{32,0},{48,16},{64,32},{80,48},{96,64},{112,80},{1... | collective-permute-start | bytes 1966088 | tf_op jit(solution)/shard_map/ppermute | solution.py:36
  28.7 13.5 %collective-permute-start.8 = (f32[2,1,1,1,1,64,1280]{6,5,4,3,2,1,0:T(8,128)S(1)}, f32[2,1,1,1,1,64,1280]{6,5,4,3,2,1,0:T(8,128)S(1)}, u32[]{:S(2)}, u32[]{:S(2)}) collective-permute-start(f32[2,1,1,1,1,64,1280]{6,5,4,3,2,1,0:T(8,128)S(1)} %get-tuple-element.78), channel_id=1, source_target_pairs={{0,16},{16,0},{32,48},{48,32},{64,80},{80,64},{96,112},{112,96},{1... | collective-permute-start | bytes 1966088 | tf_op jit(solution)/shard_map/ppermute | solution.py:36
  29.5 14.0 %collective-permute-start.5 = (f32[2,1,1,1,1,64,1280]{6,5,0,4,3,2,1:T(8,128)S(1)}, f32[2,1,1,1,1,64,1280]{6,5,0,4,3,2,1:T(8,128)S(1)}, u32[]{:S(2)}, u32[]{:S(2)}) collective-permute-start(f32[2,1,1,1,1,64,1280]{6,5,0,4,3,2,1:T(8,128)S(1)} %get-tuple-element.79), channel_id=1, source_target_pairs={{0,16},{16,0},{32,48},{48,32},{64,80},{80,64},{96,112},{112,96},{1... | collective-permute-start | bytes 1966088 | tf_op jit(solution)/shard_map/ppermute | solution.py:36
  29.6 14.0 %collective-permute-start.4 = (f32[2,1,1,1,1,64,1280]{6,5,0,4,3,2,1:T(8,128)S(1)}, f32[2,1,1,1,1,64,1280]{6,5,0,4,3,2,1:T(8,128)S(1)}, u32[]{:S(2)}, u32[]{:S(2)}) collective-permute-start(f32[2,1,1,1,1,64,1280]{6,5,0,4,3,2,1:T(8,128)S(1)} %get-tuple-element.80), channel_id=1, source_target_pairs={{0,16},{16,0},{32,48},{48,32},{64,80},{80,64},{96,112},{112,96},{1... | collective-permute-start | bytes 1966088 | tf_op jit(solution)/shard_map/ppermute | solution.py:36
  45.8 30.7 %collective-permute-start.11 = (f32[2,64,1280]{2,1,0:T(8,128)S(1)}, f32[2,64,1280]{2,1,0:T(8,128)S(1)}, u32[]{:S(2)}, u32[]{:S(2)}) collective-permute-start(f32[2,64,1280]{2,1,0:T(8,128)S(1)} %get-tuple-element.44), channel_id=1, source_target_pairs={{0,32},{16,48},{32,64},{48,80},{64,96},{80,112},{96,0},{112,16},{1... | collective-permute-start | bytes 1966088 | tf_op jit(solution)/shard_map/ppermute | solution.py:36
  45.9 30.6 %collective-permute-start.12 = (f32[2,64,1280]{2,1,0:T(8,128)S(1)}, f32[2,64,1280]{2,1,0:T(8,128)S(1)}, u32[]{:S(2)}, u32[]{:S(2)}) collective-permute-start(f32[2,64,1280]{2,1,0:T(8,128)S(1)} %get-tuple-element.45), channel_id=1, source_target_pairs={{0,96},{16,112},{32,0},{48,16},{64,32},{80,48},{96,64},{112,80},{1... | collective-permute-start | bytes 1966088 | tf_op jit(solution)/shard_map/ppermute | solution.py:36
  48.5 27.9 %collective-permute-start.15 = (f32[2,64,1280]{2,1,0:T(8,128)S(1)}, f32[2,64,1280]{2,1,0:T(8,128)S(1)}, u32[]{:S(2)}, u32[]{:S(2)}) collective-permute-start(f32[2,64,1280]{2,1,0:T(8,128)S(1)} %pad_maximum_fusion.4), channel_id=1, source_target_pairs={{0,128},{16,144},{32,160},{48,176},{64,192},{80,208},{96,224},{112... | collective-permute-start | bytes 1966088 | tf_op jit(solution)/shard_map/ppermute | solution.py:36
  53.7 15.7 %collective-permute-start.13 = (f32[64,1280]{1,0:T(8,128)S(1)}, f32[64,1280]{1,0:T(8,128)S(1)}, u32[]{:S(2)}, u32[]{:S(2)}) collective-permute-start(f32[64,1280]{1,0:T(8,128)S(1)} %get-tuple-element.46), channel_id=1, source_target_pairs={{0,64},{16,80},{32,96},{48,112},{64,0},{80,16},{96,32},{112,48},{1... | collective-permute-start | bytes 983048 | tf_op jit(solution)/shard_map/ppermute | solution.py:36
  53.7 22.7 %collective-permute-start.14 = (f32[64,1280]{1,0:T(8,128)S(1)}, f32[64,1280]{1,0:T(8,128)S(1)}, u32[]{:S(2)}, u32[]{:S(2)}) collective-permute-start(f32[64,1280]{1,0:T(8,128)S(1)} %get-tuple-element.47), channel_id=1, source_target_pairs={{0,64},{16,80},{32,96},{48,112},{64,0},{80,16},{96,32},{112,48},{1... | collective-permute-start | bytes 983048 | tf_op jit(solution)/shard_map/ppermute | solution.py:36
  122.8 24.8 %collective-permute-start.34 = (f32[2,64,1280]{2,1,0:T(8,128)S(1)}, f32[2,64,1280]{2,1,0:T(8,128)S(1)}, u32[]{:S(2)}, u32[]{:S(2)}) collective-permute-start(f32[2,64,1280]{2,1,0:T(8,128)S(1)} %multiply_subtract_fusion), channel_id=1, source_target_pairs={{0,16},{16,0},{32,48},{48,32},{64,80},{80,64},{96,112},{112,96},{1... | collective-permute-start | bytes 1966088 | tf_op jit(solution)/shard_map/ppermute | solution.py:36
  126.1 21.6 %collective-permute-start.30 = (f32[2,64,1280]{2,1,0:T(8,128)S(1)}, f32[2,64,1280]{2,1,0:T(8,128)S(1)}, u32[]{:S(2)}, u32[]{:S(2)}) collective-permute-start(f32[2,64,1280]{2,1,0:T(8,128)S(1)} %multiply_subtract_fusion), channel_id=1, source_target_pairs={{0,32},{16,48},{32,64},{48,80},{64,96},{80,112},{96,0},{112,16},{1... | collective-permute-start | bytes 1966088 | tf_op jit(solution)/shard_map/ppermute | solution.py:36
  129.1 18.6 %collective-permute-start.33 = (f32[64,1280]{1,0:T(8,128)S(1)}, f32[64,1280]{1,0:T(8,128)S(1)}, u32[]{:S(2)}, u32[]{:S(2)}) collective-permute-start(f32[64,1280]{1,0:T(8,128)S(1)} %get-tuple-element.93), channel_id=1, source_target_pairs={{0,128},{16,144},{32,160},{48,176},{64,192},{80,208},{96,224},{112... | collective-permute-start | bytes 983048 | tf_op jit(solution)/shard_map/ppermute | solution.py:36
  135.2 12.5 %collective-permute-start.31 = (f32[64,1280]{1,0:T(8,128)S(1)}, f32[64,1280]{1,0:T(8,128)S(1)}, u32[]{:S(2)}, u32[]{:S(2)}) collective-permute-start(f32[64,1280]{1,0:T(8,128)S(1)} %get-tuple-element.93), channel_id=1, source_target_pairs={{0,96},{16,112},{32,0},{48,16},{64,32},{80,48},{96,64},{112,80},{1... | collective-permute-start | bytes 983048 | tf_op jit(solution)/shard_map/ppermute | solution.py:36
  147.8 22.5 %collective-permute-start.37 = (f32[128,1280]{1,0:T(8,128)S(1)}, f32[128,1280]{1,0:T(8,128)S(1)}, u32[]{:S(2)}, u32[]{:S(2)}) collective-permute-start(f32[128,1280]{1,0:T(8,128)S(1)} %get-tuple-element.54), channel_id=1, source_target_pairs={{0,32},{16,48},{32,64},{48,80},{64,96},{80,112},{96,0},{112,16},{1... | collective-permute-start | bytes 1966088 | tf_op jit(solution)/shard_map/ppermute | solution.py:36
  147.9 22.4 %collective-permute-start.38 = (f32[128,1280]{1,0:T(8,128)S(1)}, f32[128,1280]{1,0:T(8,128)}, u32[]{:S(2)}, u32[]{:S(2)}) collective-permute-start(f32[128,1280]{1,0:T(8,128)S(1)} %get-tuple-element.55), channel_id=1, source_target_pairs={{0,96},{16,112},{32,0},{48,16},{64,32},{80,48},{96,64},{112,80},{1... | collective-permute-start | bytes 1966088 | tf_op jit(solution)/shard_map/ppermute | solution.py:36
  150.6 13.3 %collective-permute-start.40 = (f32[64,1280]{1,0:T(8,128)S(1)}, f32[64,1280]{1,0:T(8,128)}, u32[]{:S(2)}, u32[]{:S(2)}) collective-permute-start(f32[64,1280]{1,0:T(8,128)S(1)} %get-tuple-element.92), channel_id=1, source_target_pairs={{0,128},{16,144},{32,160},{48,176},{64,192},{80,208},{96,224},{112... | collective-permute-start | bytes 983048 | tf_op jit(solution)/shard_map/ppermute | solution.py:36
  155.6 14.7 %collective-permute-start.39 = (f32[64,1280]{1,0:T(8,128)S(1)}, f32[64,1280]{1,0:T(8,128)S(1)}, u32[]{:S(2)}, u32[]{:S(2)}) collective-permute-start(f32[64,1280]{1,0:T(8,128)S(1)} %collective-permute-done.33), channel_id=1, source_target_pairs={{0,64},{16,80},{32,96},{48,112},{64,0},{80,16},{96,32},{112,48},{1... | collective-permute-start | bytes 983048 | tf_op jit(solution)/shard_map/ppermute | solution.py:36
  155.6 19.8 %collective-permute-start.35 = (f32[2,64,1280]{2,1,0:T(8,128)S(1)}, f32[2,64,1280]{2,1,0:T(8,128)S(1)}, u32[]{:S(2)}, u32[]{:S(2)}) collective-permute-start(f32[2,64,1280]{2,1,0:T(8,128)S(1)} %collective-permute-done.30), channel_id=1, source_target_pairs={{0,16},{16,0},{32,48},{48,32},{64,80},{80,64},{96,112},{112,96},{1... | collective-permute-start | bytes 1966088 | tf_op jit(solution)/shard_map/ppermute | solution.py:36
  163.9 11.1 %collective-permute-start.36 = (f32[2,64,1280]{2,1,0:T(8,128)S(1)}, f32[2,64,1280]{2,1,0:T(8,128)S(1)}, u32[]{:S(2)}, u32[]{:S(2)}) collective-permute-start(f32[2,64,1280]{2,1,0:T(8,128)S(1)} %pad_maximum_fusion.5), channel_id=1, source_target_pairs={{0,16},{16,0},{32,48},{48,32},{64,80},{80,64},{96,112},{112,96},{1... | collective-permute-start | bytes 1966088 | tf_op jit(solution)/shard_map/ppermute | solution.py:36
  175.0 12.8 %collective-permute-start.46 = (f32[64,1280]{1,0:T(8,128)}, f32[64,1280]{1,0:T(8,128)}, u32[]{:S(2)}, u32[]{:S(2)}) collective-permute-start(f32[64,1280]{1,0:T(8,128)} %collective-permute-done.40), channel_id=1, source_target_pairs={{0,64},{16,80},{32,96},{48,112},{64,0},{80,16},{96,32},{112,48},{1... | collective-permute-start | bytes 983048 | tf_op jit(solution)/shard_map/ppermute | solution.py:36
  175.4 18.0 %collective-permute-start.45 = (f32[64,1280]{1,0:T(8,128)}, f32[64,1280]{1,0:T(8,128)}, u32[]{:S(2)}, u32[]{:S(2)}) collective-permute-start(f32[64,1280]{1,0:T(8,128)} %collective-permute-done.40), channel_id=1, source_target_pairs={{0,96},{16,112},{32,0},{48,16},{64,32},{80,48},{96,64},{112,80},{1... | collective-permute-start | bytes 983048 | tf_op jit(solution)/shard_map/ppermute | solution.py:36
  179.1 14.4 %collective-permute-start.44 = (f32[64,1280]{1,0:T(8,128)}, f32[64,1280]{1,0:T(8,128)}, u32[]{:S(2)}, u32[]{:S(2)}) collective-permute-start(f32[64,1280]{1,0:T(8,128)} %collective-permute-done.40), channel_id=1, source_target_pairs={{0,32},{16,48},{32,64},{48,80},{64,96},{80,112},{96,0},{112,16},{1... | collective-permute-start | bytes 983048 | tf_op jit(solution)/shard_map/ppermute | solution.py:36
  (46 other events, 696.3 us)
